TPU v7x, 128 devices: a whole 4x4x4 slice. The times are simulated.
128 devices in a mesh: token: 8 (over z, x_lo), dp: 16 (over x_hi, y, core).
Axes of the slice: x: 4 (x_hi: 2, x_lo: 2; x = x_hi * 2 + x_lo), y: 4, z: 4, core: 2. Of those that a mesh axis runs over, the one named last changes fastest.
Arguments:
- inputs: bfloat16 [16384, 16, 1024], P('dp', 'token'), may hold values from -6 to 6
- cotangent: bfloat16 [16384, 16, 1024], P('dp', 'token'), may hold values from -6 to 6
- w_gate: bfloat16 [16, 1024, 768], P('token', 'dp'), may hold values from -0.1875 to 0.1875
- w_up: bfloat16 [16, 1024, 768], P('token', 'dp'), may hold values from -0.1875 to 0.1875
- w_down: bfloat16 [16, 768, 1024], P('token', 'dp'), may hold values from -0.21875 to 0.21875
Outputs:
- grad_inputs: bfloat16 [16384, 16, 1024], P('dp', 'token')
- grad_gate: bfloat16 [16, 1024, 768], P('token', 'dp')
- grad_up: bfloat16 [16, 1024, 768], P('token', 'dp')
- grad_down: bfloat16 [16, 768, 1024], P('token', 'dp')
All inputs are finite; a program needn't handle non-finite values.
Results may differ from a plain program's by a relative error of at most 0.018.
Values may be sent and summed in bfloat16 or wider, within the bound.
A program may use at most 128 MiB of HBM per device.

v0:
```python
import math

import jax
import jax.numpy as jnp
from jax import lax
from jax.sharding import PartitionSpec as P


def side_by_side(arrays, axis, split_dim, concat_dim, along):
    both = jnp.concatenate(arrays, axis=along)
    filled, at, done = (
        lax.all_to_all(both, axis, split_axis=split_dim, concat_axis=concat_dim, tiled=True),
        0,
        [],
    )
    for a in arrays:
        done.append(lax.slice_in_dim(filled, at, at + a.shape[along], axis=along))
        at += a.shape[along]
    return tuple(done)


def in_one_piece(arrays, axis, dim, along):
    both = jnp.concatenate(arrays, axis=along)
    filled, at, done = (lax.psum_scatter(both, axis, scatter_dimension=dim, tiled=True), 0, [])
    for a in arrays:
        done.append(lax.slice_in_dim(filled, at, at + a.shape[along], axis=along))
        at += a.shape[along]
    return tuple(done)


def backward_token(mixed_in, mixed_grad, gate_w, up_w, down_w):
    gate_pre = jnp.dot(mixed_in, gate_w, preferred_element_type=jnp.float32)
    up_pre = jnp.dot(mixed_in, up_w, preferred_element_type=jnp.float32)
    sigmoid = jax.nn.sigmoid(gate_pre)
    activated = gate_pre * sigmoid
    hidden = (activated * up_pre).astype(jnp.bfloat16)
    grad_hidden = jnp.dot(mixed_grad, down_w.T, preferred_element_type=jnp.float32)
    slope = sigmoid * (1.0 + gate_pre * (1.0 - sigmoid))
    grad_gate = (grad_hidden * up_pre * slope).astype(jnp.bfloat16)
    grad_upper = (grad_hidden * activated).astype(jnp.bfloat16)
    grad_mixed = (
        jnp.dot(grad_gate, gate_w.T, preferred_element_type=jnp.float32)
        + jnp.dot(grad_upper, up_w.T, preferred_element_type=jnp.float32)
    ).astype(jnp.bfloat16)
    return (grad_mixed, grad_gate, grad_upper, hidden)


def rounded_term(left, right):
    return jnp.dot(left.T, right, preferred_element_type=jnp.float32).astype(jnp.bfloat16)


def widened(term):
    return lax.optimization_barrier(term).astype(jnp.float32)


def per_device(inputs, cotangent, w_gate, w_up, w_down):
    samples, owned, width = inputs.shape
    tokens = owned * lax.axis_size("token")
    head_width = width // tokens
    factor = 1.0 / math.sqrt(samples * lax.axis_size("dp"))

    def spread(source):
        return source.reshape(samples, owned, tokens, head_width).transpose(0, 2, 1, 3)

    mixed_all, mixed_cot = side_by_side((spread(inputs), spread(cotangent)), "token", 1, 2, 0)
    mixed_all = mixed_all.reshape(samples, owned, width)
    mixed_cot = mixed_cot.reshape(samples, owned, width)
    full_gate, full_upper, full_down = (
        lax.all_gather(w_gate, "dp", axis=1, tiled=True),
        lax.all_gather(w_up, "dp", axis=1, tiled=True),
        lax.all_gather(w_down, "dp", axis=1, tiled=True),
    )
    mixed_pieces = []
    gate_terms = []
    upper_terms = []
    down_terms = []
    for index in range(owned):
        mixed_in = mixed_all[:, index]
        mixed_grad = mixed_cot[:, index]
        grad_mixed, grad_gate, grad_upper, hidden = backward_token(
            mixed_in, mixed_grad, full_gate[index], full_upper[index], full_down[index]
        )
        mixed_pieces.append(grad_mixed)
        gate_terms.append(rounded_term(mixed_in, grad_gate))
        upper_terms.append(rounded_term(mixed_in, grad_upper))
        down_terms.append(rounded_term(hidden, mixed_grad))
    gate_stack = jnp.stack(gate_terms)
    upper_stack = jnp.stack(upper_terms)
    down_stack = jnp.stack(down_terms)
    summed = (
        *tuple(
            (
                part.astype(jnp.float32)
                for part in in_one_piece(
                    (
                        widened(gate_stack).astype(jnp.bfloat16),
                        widened(upper_stack).astype(jnp.bfloat16),
                    ),
                    "dp",
                    1,
                    0,
                )
            )
        ),
        lax.psum_scatter(
            widened(down_stack).astype(jnp.bfloat16), "dp", scatter_dimension=1, tiled=True
        ).astype(jnp.float32),
    )
    gate_total, upper_total, down_total = (summed[0], summed[1], summed[2])
    grad_gate_out = (gate_total * factor).astype(jnp.bfloat16)
    grad_upper_out = (upper_total * factor).astype(jnp.bfloat16)
    grad_down_out = (down_total * factor).astype(jnp.bfloat16)
    grad_mixed_all = jnp.stack(mixed_pieces, axis=1).reshape(samples, owned, tokens, head_width)
    returned = lax.all_to_all(grad_mixed_all, "token", split_axis=2, concat_axis=1, tiled=True)
    returned = returned.transpose(0, 2, 1, 3).reshape(samples, owned, width)
    grad_inputs = (returned.astype(jnp.float32) + cotangent.astype(jnp.float32)).astype(
        jnp.bfloat16
    )
    return (grad_inputs, grad_gate_out, grad_upper_out, grad_down_out)


def solution(mesh):
    return jax.shard_map(
        per_device,
        mesh=mesh,
        in_specs=(
            P("dp", "token", None),
            P("dp", "token", None),
            P("token", "dp", None),
            P("token", "dp", None),
            P("token", "dp", None),
        ),
        out_specs=(
            P("dp", "token", None),
            P("token", "dp", None),
            P("token", "dp", None),
            P("token", "dp", None),
        ),
        check_vma=False,
    )
```

profile of v0, /device:TPU:0, one launch (start us, length us, event | category | flops | bytes accessed | tf_op | source)
XLA Modules:
  0.0 375.7 jit_solution(15066268754435094828)
XLA Ops:
  7.2 0.0 all-gather.8.cloned.1.call-start
  7.2 0.7 all-gather.8.cloned.1.call-update
  7.9 0.0 all-gather.6.cloned.1.call-start
  7.9 0.7 all-gather.6.cloned.1.call-update
  8.6 11.1 %copy.33 = bf16[1024,2,1024]{0,2,1:T(8,128)(2,1)} copy(bf16[1024,2,1024]{2,1,0:T(2,128)(2,1)} %param.6) | data formatting | bytes 8388608 | tf_op args[1]
  19.8 11.2 %copy.32 = bf16[1024,2,1024]{0,2,1:T(8,128)(2,1)} copy(bf16[1024,2,1024]{2,1,0:T(2,128)(2,1)} %param.5) | data formatting | bytes 8388608 | tf_op args[0]
  31.0 8.2 %pad_maximum_fusion = bf16[2048,16,2,64]{0,3,1,2:T(8,128)(2,1)} fusion(bf16[1024,16,2,64]{0,3,1,2:T(8,128)(2,1)} %bitcast.119, bf16[1024,16,2,64]{0,3,1,2:T(8,128)(2,1)} %bitcast.121), kind=kLoop, calls=%fused_computation | loop fusion | flops 16777216 | bytes 16777216 | tf_op jit(solution)/shard_map/concatenate | solution.py:10
  39.1 8.3 %copy.34 = bf16[2048,16,2,64]{0,3,2,1:T(8,128)(2,1)} copy(bf16[2048,16,2,64]{0,3,1,2:T(8,128)(2,1)} %pad_maximum_fusion) | data formatting | bytes 16777216 | tf_op jit(solution)/shard_map/concatenate | solution.py:10
  47.5 6.4 %all-to-all-start = ((bf16[2048,16,2,64]{0,3,2,1:T(8,128)(2,1)}), bf16[2048,16,2,64]{0,3,2,1:T(8,128)(2,1)}, u32[]{:S(2)}, u32[]{:S(2)}) async-start(bf16[2048,16,2,64]{0,3,2,1:T(8,128)(2,1)} %copy.34), calls=%async_computation | async-start | bytes 16777216 | tf_op jit(solution)/shard_map/all_to_all | solution.py:12
  53.8 0.0 all-gather.4.cloned.1.call-start
  53.9 0.7 all-gather.4.cloned.1.call-update
  54.6 0.0 reduce-scatter.5.cloned.1.call-start
  54.6 106.3 %all-to-all-done = bf16[2048,16,2,64]{0,3,2,1:T(8,128)(2,1)} async-done(((bf16[2048,16,2,64]{0,3,2,1:T(8,128)(2,1)}), bf16[2048,16,2,64]{0,3,2,1:T(8,128)(2,1)}, u32[]{:S(2)}, u32[]{:S(2)}) %all-to-all-start) | async-done | bytes 8388640 | tf_op jit(solution)/shard_map/all_to_all | solution.py:12
  161.0 4.1 %fusion.25 = (bf16[1024,2,8,2,64]{0,4,3,1,2:T(8,128)(2,1)S(1)}, bf16[1024,2,8,2,64]{0,4,3,1,2:T(8,128)(2,1)S(1)}) fusion(bf16[2048,2,8,2,64]{0,4,3,1,2:T(8,128)(2,1)} %bitcast.5), kind=kLoop, calls=%fused_computation.57 | loop fusion | bytes 16777216 | tf_op jit(solution)/shard_map/slice | solution.py:17
  165.1 2.4 copy.35
  167.5 2.5 copy.37
  169.9 5.8 %fusion.20 = f32[1024,768]{1,0:T(8,128)} fusion(bf16[2,1024,768]{2,1,0:T(8,128)(2,1)} %all-gather.8.cloned.1.call-done, bf16[1024,2,1024]{0,2,1:T(8,128)(2,1)} %bitcast.122), kind=kOutput, calls=%fused_computation.51 | convolution fusion | flops 1610612736 | bytes 6815744 | tf_op jit(solution)/shard_map/dot_general | solution.py:32
  175.7 0.0 copy-done.1
  175.7 0.0 copy-done.6
  175.7 3.5 fusion.17
  179.2 4.0 %fusion.18 = f32[1024,768]{1,0:T(8,128)S(1)} fusion(bf16[2,1024,768]{2,1,0:T(8,128)(2,1)} %all-gather.6.cloned.1.call-done, bf16[1024,2,1024]{0,2,1:T(8,128)(2,1)} %bitcast.123), kind=kOutput, calls=%fused_computation.49 | convolution fusion | flops 1610612736 | bytes 6815744 | tf_op jit(solution)/shard_map/dot_general | solution.py:33
  183.3 0.0 copy-done.2
  183.3 0.2 copy-done.7
  183.5 1.9 fusion.15
  185.4 0.0 copy-start.12
  185.4 2.5 copy-done.4
  187.9 1.0 copy-done.14
  188.9 1.9 fusion.10
  190.8 2.1 fusion.9
  193.0 2.0 pad_maximum_fusion.5
  195.0 0.0 reduce-scatter.5.cloned.1.call-update
  195.0 0.0 reduce-scatter.3.cloned.1.call-start
  195.1 0.0 all-gather.4.cloned.1.call-done
  195.1 6.9 %multiply_convert_fusion.2 = (bf16[1024,768]{1,0:T(8,128)(2,1)S(1)}, bf16[1024,768]{1,0:T(8,128)(2,1)S(1)}) fusion(f32[1024,768]{1,0:T(8,128)} %fusion.20, f32[1024,768]{1,0:T(8,128)} %copy-done.15, bf16[2,768,1024]{2,1,0:T(8,128)(2,1)} %all-gather.4.cloned.1.call-done, bf16[1024,2,1024]{0,2,1:T(8,128)(2,1)} %bitcast.130), kind=kOutput, calls=%fused_computation.12 | convolution fusion | flops 1620836352 | bytes 13107200 | tf_op jit(solution)/shard_map/dot_general | solution.py:37
  202.0 1.8 fusion.12
  203.9 1.6 copy-done.5
  205.5 1.1 copy-done.9
  206.6 1.0 copy-done.11
  207.6 3.0 multiply_convert_fusion.4
  210.6 0.0 copy-start.17
  210.6 0.0 copy-start.21
  210.6 1.1 copy-done.17
  211.8 1.8 fusion.11
  213.6 0.3 pad_maximum_fusion.3
  213.9 1.8 fusion.14
  215.7 1.8 fusion.13
  217.5 0.3 pad_maximum_fusion.4
  217.8 3.2 pad_maximum_fusion.1
  221.0 0.0 reduce-scatter.3.cloned.1.call-update
  221.0 3.3 fusion.19
  224.4 1.8 fusion.16
  226.2 0.0 copy-done.8
  226.2 0.5 copy-done.20
  226.7 1.9 add_convert_fusion
  228.6 1.8 add_convert_fusion.1
  230.4 0.4 pad_maximum_fusion.2
  230.8 56.8 %all_to_all.27 = bf16[1024,2,16,64]{0,3,1,2:T(8,128)(2,1)S(1)} all-to-all(bf16[1024,2,16,64]{0,3,1,2:T(8,128)(2,1)S(1)} %pad_maximum_fusion.2), channel_id=1, replica_groups=mesh['token'=8,'dp'=16] {'token'}, dimensions={2} | all-to-all | bytes 8388608 | tf_op jit(solution)/shard_map/all_to_all | solution.py:114
  287.6 1.1 copy.43
  288.7 1.4 copy-done
  290.1 3.7 fusion
  293.8 11.5 %copy.45 = bf16[1024,2,1024]{2,1,0:T(2,128)(2,1)} copy(bf16[1024,2,1024]{0,2,1:T(8,128)(2,1)} %fusion) | data formatting | bytes 8388608
  305.3 1.6 multiply_convert_fusion.12
  306.9 60.4 %reduce-scatter.3.cloned.1.call-done = bf16[4,64,768]{2,1,0:T(8,128)(2,1)} async-done(((bf16[4,1024,768]{2,1,0:T(8,128)(2,1)}), bf16[4,64,768]{2,1,0:T(8,128)(2,1)}) %reduce-scatter.3.cloned.1.call-update) | async-done | bytes 393232 | tf_op jit(solution)/shard_map/reduce_scatter | solution.py:24
  367.4 1.8 multiply_convert_fusion.13
  (33 shorter events, 0.1 us)
Async XLA Ops:
  7.2 162.8 %all-gather.8.cloned.1.call-start = ((), (), s32[]{:S(2)}) async-start(), calls=%async_computation.6 | async-start | bytes 3342336 | tf_op jit(solution)/shard_map/all_gather | solution.py:69
  7.9 171.3 %all-gather.6.cloned.1.call-start = ((), (), s32[]{:S(2)}) async-start(), calls=%async_computation.5 | async-start | bytes 3342336 | tf_op jit(solution)/shard_map/all_gather | solution.py:70
  47.5 113.5 %all-to-all-start = ((bf16[2048,16,2,64]{0,3,2,1:T(8,128)(2,1)}), bf16[2048,16,2,64]{0,3,2,1:T(8,128)(2,1)}, u32[]{:S(2)}, u32[]{:S(2)}) async-start(bf16[2048,16,2,64]{0,3,2,1:T(8,128)(2,1)} %copy.34), calls=%async_computation | async-start | bytes 16777216 | tf_op jit(solution)/shard_map/all_to_all | solution.py:12
  53.8 141.2 %all-gather.4.cloned.1.call-start = ((), (), s32[]{:S(2)}) async-start(), calls=%async_computation.4 | async-start | bytes 3342336 | tf_op jit(solution)/shard_map/all_gather | solution.py:71
  54.6 250.7 %reduce-scatter.5.cloned.1.call-start = ((), (), s32[]{:S(2)}) async-start(), calls=%async_computation.8 | async-start | bytes 3342336 | tf_op jit(solution)/shard_map/reduce_scatter | solution.py:105
  169.9 5.8 %copy-start.1 = (bf16[1024,2,8,2,64]{0,4,3,2,1:T(8,128)(2,1)S(1)}, bf16[1024,2,8,2,64]{0,4,3,2,1:T(8,128)(2,1)}, u32[]{:S(2)}) copy-start(bf16[1024,2,8,2,64]{0,4,3,2,1:T(8,128)(2,1)} %copy.37) | copy-start | bytes 12582916
  169.9 5.8 %copy-start.6 = (bf16[2,1024,768]{2,1,0:T(8,128)(2,1)S(1)}, bf16[2,1024,768]{2,1,0:T(8,128)(2,1)}, u32[]{:S(2)}) copy-start(bf16[2,1024,768]{2,1,0:T(8,128)(2,1)} %all-gather.8.cloned.1.call-done) | copy-start | bytes 9437188
  179.2 4.1 %copy-start.2 = (bf16[1024,2,8,2,64]{0,4,3,2,1:T(8,128)(2,1)S(1)}, bf16[1024,2,8,2,64]{0,4,3,2,1:T(8,128)(2,1)}, u32[]{:S(2)}) copy-start(bf16[1024,2,8,2,64]{0,4,3,2,1:T(8,128)(2,1)} %copy.37) | copy-start | bytes 12582916
  179.2 4.3 %copy-start.7 = (bf16[2,1024,768]{2,1,0:T(8,128)(2,1)S(1)}, bf16[2,1024,768]{2,1,0:T(8,128)(2,1)}, u32[]{:S(2)}) copy-start(bf16[2,1024,768]{2,1,0:T(8,128)(2,1)} %all-gather.6.cloned.1.call-done) | copy-start | bytes 9437188
  183.5 1.9 copy-start.15
  183.5 4.4 %copy-start.4 = (bf16[1024,2,8,2,64]{0,4,3,2,1:T(8,128)(2,1)S(1)}, bf16[1024,2,8,2,64]{0,4,3,2,1:T(8,128)(2,1)}, u32[]{:S(2)}) copy-start(bf16[1024,2,8,2,64]{0,4,3,2,1:T(8,128)(2,1)} %copy.35) | copy-start | bytes 12582916
  183.5 5.4 %copy-start.14 = (f32[1024,768]{1,0:T(8,128)S(1)}, f32[1024,768]{1,0:T(8,128)}, u32[]{:S(2)}) copy-start(f32[1024,768]{1,0:T(8,128)} %fusion.20) | copy-start | bytes 9437188
  185.4 5.4 %copy-start.12 = (f32[1024,768]{1,0:T(8,128)}, f32[1024,768]{1,0:T(8,128)S(1)}, u32[]{:S(2)}) copy-start(f32[1024,768]{1,0:T(8,128)S(1)} %fusion.15) | copy-start | bytes 9437188
  188.9 1.9 copy-start.10
  195.0 172.4 %reduce-scatter.3.cloned.1.call-start = ((), (), s32[]{:S(2)}) async-start(), calls=%async_computation.7 | async-start | bytes 6684672 | tf_op jit(solution)/shard_map/reduce_scatter | solution.py:24
  195.1 6.9 %copy-start.3 = (bf16[1024,2,8,2,64]{0,4,3,2,1:T(8,128)(2,1)S(1)}, bf16[1024,2,8,2,64]{0,4,3,2,1:T(8,128)(2,1)}, u32[]{:S(2)}) copy-start(bf16[1024,2,8,2,64]{0,4,3,2,1:T(8,128)(2,1)} %copy.37) | copy-start | bytes 12582916
  195.1 8.8 %copy-start.13 = (f32[1024,768]{1,0:T(8,128)S(1)}, f32[1024,768]{1,0:T(8,128)}, u32[]{:S(2)}) copy-start(f32[1024,768]{1,0:T(8,128)} %copy-done.12) | copy-start | bytes 9437188
  202.0 1.9 copy-start.16
  202.0 11.9 %copy-start.19 = (bf16[1024,768]{1,0:T(8,128)(2,1)}, bf16[1024,768]{1,0:T(8,128)(2,1)S(1)}, u32[]{:S(2)}) copy-start(bf16[1024,768]{1,0:T(8,128)(2,1)S(1)} %get-tuple-element.20) | copy-start | bytes 4718596
  202.0 3.5 copy-start.5
  202.0 4.5 %copy-start.9 = (bf16[2,768,1024]{2,1,0:T(8,128)(2,1)S(1)}, bf16[2,768,1024]{2,1,0:T(8,128)(2,1)}, u32[]{:S(2)}) copy-start(bf16[2,768,1024]{2,1,0:T(8,128)(2,1)} %all-gather.4.cloned.1.call-done) | copy-start | bytes 9437188
  202.0 5.6 %copy-start.11 = (f32[1024,768]{1,0:T(8,128)S(1)}, f32[1024,768]{1,0:T(8,128)}, u32[]{:S(2)}) copy-start(f32[1024,768]{1,0:T(8,128)} %fusion.17) | copy-start | bytes 9437188
  210.6 1.2 copy-start.17
  210.6 5.1 %copy-start.21 = (bf16[1024,768]{1,0:T(8,128)(2,1)}, bf16[1024,768]{1,0:T(8,128)(2,1)S(1)}, u32[]{:S(2)}) copy-start(bf16[1024,768]{1,0:T(8,128)(2,1)S(1)} %get-tuple-element.18) | copy-start | bytes 4718596
  221.0 3.4 copy-start.18
  224.3 1.9 copy-start.8
  224.4 2.3 copy-start.20
  226.7 1.9 copy-start.22
  287.6 2.5 copy-start
Sparse Core Ops, SparseCore 0:
  10.5 52.9 all-gather.7
  66.0 59.9 all-gather.5
  128.6 50.5 all-gather.3
  195.1 79.5 reduce-scatter.4
  278.7 88.5 reduce-scatter.2
where the time goes:
time: 377 us; the launch traced here: 376 us
  waiting for transfers between devices  169 us (45%)
  local copies, waits for them, and re-layouts  62.7 us (17%)
  blocking collectives  56.8 us (15%)
  matrix products  45.2 us (12%)
  other arithmetic  21.5 us (6%)
  between operations  14.1 us (4%)
  starting transfers between devices  6.56 us (2%)
    all_to_all x1, waiting for transfers between devices, side_by_side(): lax.all_to_all(both, axis, split_axis=split_dim, concat_axis=concat_dim,...  106 us
    reduce_scatter x1, waiting for transfers between devices, in_one_piece(): lax.psum_scatter(both, axis, scatter_dimension=dim, tiled=True)  60.4 us
    all_to_all x1, blocking collectives, per_device(): lax.all_to_all(grad_mixed_all, 'token', split_axis=2, concat_axis=1, tile...  56.8 us
    unnamed x49, local copies, waits for them, and re-layouts  44.3 us
    dot_general x6, matrix products, rounded_term(): jnp.dot(left.T, right, preferred_element_type=jnp.float32)  11.2 us
    dot_general x2, matrix products, backward_token(): jnp.dot(mixed_grad, down_w.T, preferred_element_type=jnp.float32)  9.91 us
    dot_general x2, matrix products, backward_token(): gate_pre = jnp.dot(mixed_in, gate_w, preferred_element_type=jnp.float32)  9.26 us
    slice x3, local copies, waits for them, and re-layouts, side_by_side(): done.append(lax.slice_in_dim(filled, at, at + a.shape[along], axis=along))  8.98 us
  transfers between devices with their start and end apart: 6, of which 2 were waited for; matrix products, arithmetic and copies ran while one was open for 31% of the time, Pallas kernels for 0%

commit v1 on v0

v1 whole, which is shorter than its diff:
```python
import functools

import jax
import jax.numpy as jnp
from jax import lax
from jax.experimental import pallas as pl
from jax.experimental.pallas import tpu as pltpu
from jax.sharding import PartitionSpec as P

MESH = pl.DeviceIdType.MESH
BF = jnp.bfloat16
F32 = jnp.float32
LANES = 128
HALF = 64
TOKEN_DEVICES = 8
DP = 16
ROWS = 128
BLOCK = 256


def nn(a, b):
    return jnp.dot(a, b, preferred_element_type=F32)


def nt(a, b):
    return lax.dot_general(a, b, (((1,), (1,)), ((), ())), preferred_element_type=F32)


def tn(a, b):
    return lax.dot_general(a, b, (((0,), (0,)), ((), ())), preferred_element_type=F32)


def halves(a, b):
    low = jnp.concatenate([a[:, :HALF], b[:, :HALF]], axis=1)
    high = jnp.concatenate([a[:, HALF:], b[:, HALF:]], axis=1)
    return low, high


def kernel(
    factor,
    x, g, w_gate, w_up, w_down,
    out, out_gate, out_up, out_down,
    x_raw, g_raw, stage, mixed, full_gate, full_up, full_down,
    hid, g_gate, g_up, tmp,
    p_gate, p_up, p_down,
    c_gate, c_up, c_down,
    y_gate, y_up, y_down,
    s_gate, s_up, s_down,
    r_gate, r_up, r_down,
    back,
    load_sem, own_sem, wload_sem, in_send, in_recv, out_send, out_recv, own_out_sem, write_sem,
    ag_send, ag_recv, rs1_send, rs1_recv, rs2_send, rs2_recv, rs3_send, rs3_recv,
):
    samples = x.shape[0]
    me = lax.axis_index("token")
    z, xl = me // 2, me % 2
    d = lax.axis_index("dp")
    xh, y, c = d // 8, (d // 2) % 4, d % 2

    def dp_of(xh_, y_, c_):
        return xh_ * 8 + y_ * 2 + c_

    def partner(i):
        return ((z + i // 2) % 4) * 2 + (xl + i % 2) % 2

    def inverse(i):
        return ((4 - i // 2) % 4) * 2 + i % 2

    def columns(q):
        return pl.ds(pl.multiple_of(q * LANES, LANES), LANES)

    def remote(src, dst, send, recv, token_to, dp_to):
        return pltpu.make_async_remote_copy(
            src_ref=src, dst_ref=dst, send_sem=send, recv_sem=recv,
            device_id=(token_to, dp_to), device_id_type=MESH,
        )

    def load(i, which):
        src, dst = ((x, x_raw), (g, g_raw))[which]
        return pltpu.make_async_copy(
            src.at[:, :, columns(partner(i))], dst.at[i], load_sem.at[which, i]
        )

    def start_loads(i, _):
        load(i, 0).start()
        load(i, 1).start()
        return 0

    lax.fori_loop(1, TOKEN_DEVICES, start_loads, 0)
    start_loads(0, 0)
    own_weights = [
        pltpu.make_async_copy(src, dst.at[:, d], wload_sem.at[n])
        for n, (src, dst) in enumerate(
            ((w_gate, full_gate), (w_up, full_up), (w_down, full_down))
        )
    ]
    for copy in own_weights:
        copy.start()

    barrier = pltpu.get_barrier_semaphore()

    def greet(i, _):
        pl.semaphore_signal(barrier, inc=1, device_id=(partner(i), d), device_id_type=MESH)
        return 0

    lax.fori_loop(1, TOKEN_DEVICES, greet, 0)
    for to in (
        dp_of(xh, (y + 1) % 4, c),
        dp_of(xh, (y + 2) % 4, c),
        dp_of(xh, (y + 3) % 4, c),
        dp_of(1 - xh, y, c),
        dp_of(xh, y, 1 - c),
    ):
        pl.semaphore_signal(barrier, inc=1, device_id=(me, to), device_id_type=MESH)
    pl.semaphore_wait(barrier, 12)

    fulls = (full_gate, full_up, full_down)
    mine = (w_gate, w_up, w_down)
    d_x = dp_of(1 - xh, y, c)
    d_c = dp_of(xh, y, 1 - c)

    def gather(slot, shard, to, srcs=None):
        return [
            remote(
                (srcs[n] if srcs else fulls[n].at[:, shard]), fulls[n].at[:, shard],
                ag_send.at[slot, n], ag_recv.at[slot, n], me, to,
            )
            for n in range(3)
        ]

    ag_own_x = gather(0, d, d_x, mine)
    ag_own_y = [gather(dy, d, dp_of(xh, (y + dy) % 4, c), mine) for dy in (1, 2, 3)]
    ag_own_c = gather(4, d, d_c, mine)
    ag_far_y = [gather(4 + dy, d_x, dp_of(xh, (y + dy) % 4, c)) for dy in (1, 2, 3)]
    ag_far_c = gather(8, d_x, d_c)
    ag_pass_own = [gather(8 + dy, dp_of(xh, (y + 4 - dy) % 4, c), d_c) for dy in (1, 2, 3)]
    ag_pass_far = [gather(11 + dy, dp_of(1 - xh, (y + 4 - dy) % 4, c), d_c) for dy in (1, 2, 3)]

    def start_all(copies):
        for copy in copies:
            copy.start()

    start_all(ag_own_x)
    for copies in ag_own_y:
        start_all(copies)
    start_all(ag_own_c)

    def incoming(token, which, i):
        return remote(
            stage.at[token, which, i], mixed.at[token, which, :, columns(me)],
            in_send.at[token, which, i], in_recv.at[token, which, i], partner(i), d,
        )

    def shuffle(i, which):
        load(i, which).wait()
        raw = ((x_raw, g_raw)[which]).at[i].reshape(2 * samples, LANES)

        def step(k, _):
            row = pl.multiple_of(k * ROWS, ROWS)
            tmp[...] = raw[pl.ds(2 * row, 2 * ROWS), :].astype(F32)
            low, high = halves(tmp[pl.ds(0, ROWS, stride=2), :], tmp[pl.ds(1, ROWS, stride=2), :])
            stage[0, which, i, pl.ds(row, ROWS), :] = low.astype(BF)
            stage[1, which, i, pl.ds(row, ROWS), :] = high.astype(BF)
            return 0

        lax.fori_loop(0, samples // ROWS, step, 0)

    def send_in(i, _):
        shuffle(i, 0)

        @pl.when(i > 1)
        def _():
            incoming(0, 1, i - 1).start()

        shuffle(i, 1)
        incoming(0, 0, i).start()
        return 0

    lax.fori_loop(1, TOKEN_DEVICES, send_in, 0)
    shuffle(0, 0)
    incoming(0, 1, TOKEN_DEVICES - 1).start()
    shuffle(0, 1)

    def send_in_b(i, _):
        incoming(1, 0, i).start()
        incoming(1, 1, i).start()
        return 0

    lax.fori_loop(1, TOKEN_DEVICES, send_in_b, 0)
    own_in = [
        pltpu.make_async_copy(
            stage.at[token, which, 0], mixed.at[token, which, :, columns(me)], own_sem.at[token, which]
        )
        for token in range(2)
        for which in range(2)
    ]
    start_all(own_in)

    for copy in ag_own_x:
        copy.wait()
    for copies in ag_far_y:
        start_all(copies)
    start_all(ag_far_c)
    for n in range(3):
        for copy in ag_own_y[n]:
            copy.wait()
        start_all(ag_pass_own[n])
    for n in range(3):
        for copy in ag_far_y[n]:
            copy.wait()
        start_all(ag_pass_far[n])
    for copies in (ag_own_c, ag_far_c, *ag_pass_own, *ag_pass_far):
        for copy in copies:
            copy.wait()
    for copy in (*own_weights, *own_in):
        copy.wait()

    parts = (p_gate, p_up, p_down)
    cores = (c_gate, c_up, c_down)
    over_y = (y_gate, y_up, y_down)
    sums = (s_gate, s_up, s_down)
    over_x = (r_gate, r_up, r_down)
    results = (out_gate, out_up, out_down)

    def rs1(token):
        return [
            remote(
                parts[n].at[:, :, 1 - c], cores[n].at[token],
                rs1_send.at[token, n], rs1_recv.at[token, n], me, d_c,
            )
            for n in range(3)
        ]

    def rs2(token):
        return [
            remote(
                cores[n].at[token, :, (y + dy) % 4], over_y[n].at[token, dy - 1],
                rs2_send.at[token, dy - 1, n], rs2_recv.at[token, dy - 1, n],
                me, dp_of(xh, (y + dy) % 4, c),
            )
            for dy in (1, 2, 3)
            for n in range(3)
        ]

    def rs3(token):
        return [
            remote(
                sums[n].at[token], over_x[n].at[token],
                rs3_send.at[token, n], rs3_recv.at[token, n], me, d_x,
            )
            for n in range(3)
        ]

    def outgoing(token, i):
        return remote(
            stage.at[token, 0, partner(i)], back.at[token, me],
            out_send.at[token, i], out_recv.at[token, i], partner(i), d,
        )

    def own_back(token):
        return pltpu.make_async_copy(
            stage.at[token, 0, me], back.at[token, me], own_out_sem.at[token]
        )

    def wait_in(token):
        def body(i, _):
            incoming(token, 0, i).wait()
            incoming(token, 1, i).wait()
            return 0

        lax.fori_loop(1, TOKEN_DEVICES, body, 0)

    def weight(n, token):
        full = fulls[n]
        return full[token].reshape(full.shape[1] * full.shape[2], full.shape[3])

    def forward(token):
        def step(i, _):
            r = pl.ds(pl.multiple_of(i * BLOCK, BLOCK), BLOCK)
            rows = mixed[token, 0, r, :]
            gate = nn(rows, weight(0, token))
            up = nn(rows, weight(1, token))
            grad = nt(mixed[token, 1, r, :], weight(2, token))
            sig = jax.nn.sigmoid(gate)
            act = gate * sig
            hid[r, :] = (act * up).astype(BF)
            g_gate[r, :] = (grad * up * (sig * (1.0 + gate * (1.0 - sig)))).astype(BF)
            g_up[r, :] = (grad * act).astype(BF)
            return 0

        lax.fori_loop(0, samples // BLOCK, step, 0)

    def weight_terms(token):
        def step(i, _):
            left = mixed[token, 0, :, pl.ds(pl.multiple_of(i * BLOCK, BLOCK), BLOCK)]
            at = pl.ds((i % 2) * 2, 2)
            p_gate[i // 2, at] = tn(left, g_gate[...]).astype(BF).reshape(2, 2, *p_gate.shape[3:])
            p_up[i // 2, at] = tn(left, g_up[...]).astype(BF).reshape(2, 2, *p_up.shape[3:])
            return 0

        lax.fori_loop(0, 4, step, 0)
        cut = hid.shape[1] // 2

        def step_down(i, _):
            left = hid[:, pl.ds(pl.multiple_of(i * cut, LANES), cut)]
            p_down[i] = tn(left, mixed[token, 1]).astype(BF).reshape(p_down.shape[1:])
            return 0

        lax.fori_loop(0, 2, step_down, 0)

    def backward(token):
        def step(i, _):
            r = pl.ds(pl.multiple_of(i * BLOCK, BLOCK), BLOCK)
            v = (nt(g_gate[r, :], weight(0, token)) + nt(g_up[r, :], weight(1, token))).astype(BF)
            for q in range(TOKEN_DEVICES):
                stage[token, 0, q, r, :] = v[:, q * LANES : (q + 1) * LANES]
            return 0

        lax.fori_loop(0, samples // BLOCK, step, 0)

    def core_sum(token):
        def step(k, _):
            a, b = k // 4, k % 4
            for n in range(3):
                total = parts[n][a, b, c].astype(F32) + cores[n][token, a, b].astype(F32)
                cores[n][token, a, b] = total.astype(BF)
            return 0

        lax.fori_loop(0, 8, step, 0)

    def y_sum(n, token, at):
        total = cores[n][token, at, y].astype(F32)
        for dy in range(3):
            total = total + over_y[n][token, dy, at].astype(F32)
        return total

    def y_stage(token):
        for copy in rs2(token):
            copy.wait()
        for n in range(3):
            sums[n][token] = y_sum(n, token, 1 - xh).astype(BF)

    def x_stage(token):
        for copy in rs3(token):
            copy.wait()
        for n in range(3):
            total = y_sum(n, token, xh) + over_x[n][token].astype(F32)
            results[n][token] = (total * factor).astype(BF)

    def compute(token):
        forward(token)
        if token == 1:
            for copy in first_terms:
                copy.wait_send()
            y_stage(0)
            start_all(rs3(0))
        weight_terms(token)
        backward(token)
        terms = rs1(token)
        start_all(terms)

        def send_back(i, _):
            outgoing(token, i).start()
            return 0

        lax.fori_loop(1, TOKEN_DEVICES, send_back, 0)
        own_back(token).start()
        for copy in terms:
            copy.wait_recv()
        core_sum(token)
        start_all(rs2(token))
        return terms

    wait_in(0)
    first_terms = compute(0)
    wait_in(1)
    second_terms = compute(1)
    x_stage(0)

    def write(i):
        return pltpu.make_async_copy(
            x_raw.at[i], out.at[:, :, columns(partner(i))], write_sem.at[i]
        )

    def finish(i):
        q = partner(i)
        cot = g_raw.at[i].reshape(2 * samples, LANES)
        target = x_raw.at[i].reshape(2 * samples, LANES)

        def step(k, _):
            row = pl.multiple_of(k * ROWS, ROWS)
            even, odd = halves(
                back[0, q, pl.ds(row, ROWS), :].astype(F32), back[1, q, pl.ds(row, ROWS), :].astype(F32)
            )
            tmp[pl.ds(0, ROWS, stride=2), :] = even
            tmp[pl.ds(1, ROWS, stride=2), :] = odd
            both = pl.ds(2 * row, 2 * ROWS)
            target[both, :] = (tmp[...] + cot[both, :].astype(F32)).astype(BF)
            return 0

        lax.fori_loop(0, samples // ROWS, step, 0)
        write(i).start()

    own_back(0).wait()
    own_back(1).wait()
    finish(0)

    def take_back(i, _):
        outgoing(0, inverse(i)).wait_recv()
        outgoing(1, inverse(i)).wait_recv()
        finish(i)
        return 0

    lax.fori_loop(1, 5, take_back, 0)
    y_stage(1)
    start_all(rs3(1))
    lax.fori_loop(5, TOKEN_DEVICES, take_back, 0)
    x_stage(1)
    for copy in second_terms:
        copy.wait_send()

    def drain(i, _):
        outgoing(0, i).wait_send()
        outgoing(1, i).wait_send()
        write(i).wait()
        return 0

    lax.fori_loop(1, TOKEN_DEVICES, drain, 0)
    write(0).wait()


def solution(mesh):
    def per_device(inputs, cotangent, w_gate, w_up, w_down):
        samples, owned, width = inputs.shape
        up_rows, ff = w_gate.shape[1:]
        down_rows = w_down.shape[1]
        factor = float(samples * DP) ** -0.5
        anywhere = pl.BlockSpec(memory_space=pl.ANY)
        vmem = pl.BlockSpec(memory_space=pltpu.VMEM)
        dma = pltpu.SemaphoreType.DMA

        def three(*lead):
            return [
                pltpu.VMEM((*lead, up_rows, ff), BF),
                pltpu.VMEM((*lead, up_rows, ff), BF),
                pltpu.VMEM((*lead, down_rows, width), BF),
            ]

        raw = pltpu.VMEM((TOKEN_DEVICES, samples, owned, LANES), BF)
        hidden = pltpu.VMEM((samples, ff), BF)
        return pl.pallas_call(
            functools.partial(kernel, factor),
            name="mixer_backward",
            out_shape=(
                jax.ShapeDtypeStruct(inputs.shape, BF),
                jax.ShapeDtypeStruct(w_gate.shape, BF),
                jax.ShapeDtypeStruct(w_up.shape, BF),
                jax.ShapeDtypeStruct(w_down.shape, BF),
            ),
            in_specs=[anywhere] * 5,
            out_specs=(anywhere, vmem, vmem, vmem),
            scratch_shapes=[
                raw, raw,
                pltpu.VMEM((2, 2, TOKEN_DEVICES, samples, LANES), BF),
                pltpu.VMEM((2, 2, samples, width), BF),
                *three(2, DP),
                hidden, hidden, hidden,
                pltpu.VMEM((2 * ROWS, LANES), F32),
                *three(2, 4, 2),
                *three(2, 2, 4),
                *three(2, 3, 2),
                *three(2),
                *three(2),
                pltpu.VMEM((2, TOKEN_DEVICES, samples, LANES), BF),
                dma((2, TOKEN_DEVICES)), dma((2, 2)), dma((3,)),
                dma((2, 2, TOKEN_DEVICES)), dma((2, 2, TOKEN_DEVICES)),
                dma((2, TOKEN_DEVICES)), dma((2, TOKEN_DEVICES)), dma((2,)), dma((TOKEN_DEVICES,)),
                dma((15, 3)), dma((15, 3)),
                dma((2, 3)), dma((2, 3)), dma((2, 3, 3)), dma((2, 3, 3)), dma((2, 3)), dma((2, 3)),
            ],
            compiler_params=pltpu.CompilerParams(
                collective_id=0, has_side_effects=True, vmem_limit_bytes=67_000_000
            ),
        )(inputs, cotangent, w_gate, w_up, w_down)

    return jax.shard_map(
        per_device,
        mesh=mesh,
        in_specs=(
            P("dp", "token", None),
            P("dp", "token", None),
            P("token", "dp", None),
            P("token", "dp", None),
            P("token", "dp", None),
        ),
        out_specs=(
            P("dp", "token", None),
            P("token", "dp", None),
            P("token", "dp", None),
            P("token", "dp", None),
        ),
        check_vma=False,
    )
```

time: 377 us -> 188 us (0.50)
  Pallas kernels: 0 us -> 178 us
  waiting for transfers between devices: 169 us -> 0 us
  blocking collectives: 56.8 us -> 0 us
  local copies, waits for them, and re-layouts: 62.7 us -> 9.18 us
  matrix products: 45.2 us -> 0 us
  other arithmetic: 21.5 us -> 0 us
  between operations: 14.1 us -> 0.67 us
  starting transfers between devices: 6.56 us -> 0 us
    pallas_call x0 -> x1, Pallas kernels: none -> 178 us  [per_device(): pl.pallas_call(functools.partial(kernel, factor), name='mixer_backward',...]
    all_to_all x1 -> x0, waiting for transfers between devices: 106 us -> none  [side_by_side(): lax.all_to_all(both, axis, split_axis=split_dim, concat_axis=concat_dim,...]
    reduce_scatter x2 -> x0, waiting for transfers between devices: 60.4 us -> none  [the longest x1 60.4 us: in_one_piece(): lax.psum_scatter(both, axis, scatter_dimension=dim, tiled=True)]
    all_to_all x1 -> x0, blocking collectives: 56.8 us -> none  [per_device(): lax.all_to_all(grad_mixed_all, 'token', split_axis=2, concat_axis=1, tile...]
    dot_general x16 -> x0, matrix products: 45.2 us -> none  [the longest x6 11.2 us: rounded_term(): jnp.dot(left.T, right, preferred_element_type=jnp.float32)]
    unnamed x49 -> x10, local copies, waits for them, and re-layouts: 44.3 us -> 9.18 us
    concatenate x2 -> x0, other arithmetic: 11.4 us -> none  [the longest x1 8.19 us: side_by_side(): both = jnp.concatenate(arrays, axis=along)]
    slice x3 -> x0, local copies, waits for them, and re-layouts: 8.98 us -> none  [side_by_side(): done.append(lax.slice_in_dim(filled, at, at + a.shape[along], axis=along))]
  transfers between devices with their start and end apart: 6 -> 0, of which waited for: 2 -> 0; matrix products, arithmetic and copies ran while one was open for 31% -> 0% of each run, Pallas kernels for 0% -> 0%
where the time goes in v1:
time: 188 us
  Pallas kernels  178 us (95%)
  local copies, waits for them, and re-layouts  9.18 us (5%)
    pallas_call x1, Pallas kernels, per_device(): pl.pallas_call(functools.partial(kernel, factor), name='mixer_backward',...  178 us
    unnamed x10, local copies, waits for them, and re-layouts  9.18 us

profile of v1, /device:TPU:0, one launch (start us, length us, event | category | flops | bytes accessed | tf_op | source)
XLA Modules:
  0.0 187.8 jit_solution(17226116719654465050)
XLA Ops:
  0.6 178.0 %mixer_backward.1 = (bf16[1024,2,1024]{2,1,0:T(2,128)(2,1)}, bf16[2,64,768]{2,1,0:T(8,128)(2,1)}, bf16[2,64,768]{2,1,0:T(8,128)(2,1)}, bf16[2,48,1024]{2,1,0:T(8,128)(2,1)}) custom-call(bf16[1024,2,1024]{2,1,0:T(2,128)(2,1)} %x.1, bf16[1024,2,1024]{2,1,0:T(2,128)(2,1)} %g.1, bf16[2,64,768]{2,1,0:T(8,128)(2,1)} %w_gate.1, bf16[2,64,768]{2,1,0:T(8,128)(2,1)} %w_up.1, ...), custom_call_target="tpu_custom_call" | custom-call | tf_op jit(solution)/shard_map/mixer_backward/pallas_call | solution.py:451
  178.6 0.0 copy-start.2
  178.6 0.0 copy-start.1
  178.6 0.0 copy-start
  178.6 7.1 %copy.13 = bf16[1024,2,1024]{2,1,0:T(2,128)(2,1)} copy(bf16[1024,2,1024]{2,1,0:T(2,128)(2,1)} %get-tuple-element.8) | data formatting | bytes 8388608
  185.8 0.0 copy-done.2
  185.8 0.7 copy.14
  186.5 0.0 copy-done.1
  186.5 0.7 copy.15
  187.1 0.0 copy-done
  187.1 0.7 copy.16
Async XLA Ops:
  178.6 7.2 %copy-start.2 = (bf16[2,64,768]{2,1,0:T(8,128)(2,1)S(1)}, bf16[2,64,768]{2,1,0:T(8,128)(2,1)}, u32[]{:S(2)}) copy-start(bf16[2,64,768]{2,1,0:T(8,128)(2,1)} %get-tuple-element.9) | copy-start | bytes 589828
  178.6 7.8 %copy-start.1 = (bf16[2,64,768]{2,1,0:T(8,128)(2,1)S(1)}, bf16[2,64,768]{2,1,0:T(8,128)(2,1)}, u32[]{:S(2)}) copy-start(bf16[2,64,768]{2,1,0:T(8,128)(2,1)} %get-tuple-element.10) | copy-start | bytes 589828
  178.6 8.5 %copy-start = (bf16[2,48,1024]{2,1,0:T(8,128)(2,1)S(1)}, bf16[2,48,1024]{2,1,0:T(8,128)(2,1)}, u32[]{:S(2)}) copy-start(bf16[2,48,1024]{2,1,0:T(8,128)(2,1)} %get-tuple-element.11) | copy-start | bytes 589828

commit v2 on v1

--- a/solution.py
+++ b/solution.py
@@ -16,6 +16,8 @@
 DP = 16
 ROWS = 128
 BLOCK = 256
+UNROLL = 4
+PIECES = 4
 
 
 def nn(a, b):
@@ -31,9 +33,9 @@
 
 
 def halves(a, b):
-    low = jnp.concatenate([a[:, :HALF], b[:, :HALF]], axis=1)
-    high = jnp.concatenate([a[:, HALF:], b[:, HALF:]], axis=1)
-    return low, high
+    first = lax.broadcasted_iota(jnp.int32, a.shape, 1) < HALF
+    turned = pltpu.roll(jnp.where(first, b, a), HALF, 1)
+    return jnp.where(first, a, turned), jnp.where(first, turned, b)
 
 
 def kernel(
@@ -156,14 +158,18 @@
         raw = ((x_raw, g_raw)[which]).at[i].reshape(2 * samples, LANES)
 
         def step(k, _):
-            row = pl.multiple_of(k * ROWS, ROWS)
-            tmp[...] = raw[pl.ds(2 * row, 2 * ROWS), :].astype(F32)
-            low, high = halves(tmp[pl.ds(0, ROWS, stride=2), :], tmp[pl.ds(1, ROWS, stride=2), :])
-            stage[0, which, i, pl.ds(row, ROWS), :] = low.astype(BF)
-            stage[1, which, i, pl.ds(row, ROWS), :] = high.astype(BF)
-            return 0
-
-        lax.fori_loop(0, samples // ROWS, step, 0)
+            rows = [pl.multiple_of((k * UNROLL + u) * ROWS, ROWS) for u in range(UNROLL)]
+            for u, row in enumerate(rows):
+                tmp[u] = raw[pl.ds(2 * row, 2 * ROWS), :].astype(F32)
+            for u, row in enumerate(rows):
+                low, high = halves(
+                    tmp[u, pl.ds(0, ROWS, stride=2), :], tmp[u, pl.ds(1, ROWS, stride=2), :]
+                )
+                stage[0, which, i, pl.ds(row, ROWS), :] = low.astype(BF)
+                stage[1, which, i, pl.ds(row, ROWS), :] = high.astype(BF)
+            return 0
+
+        lax.fori_loop(0, samples // (ROWS * UNROLL), step, 0)
 
     def send_in(i, _):
         shuffle(i, 0)
@@ -222,16 +228,13 @@
     over_x = (r_gate, r_up, r_down)
     results = (out_gate, out_up, out_down)
 
-    def rs1(token):
-        return [
-            remote(
-                parts[n].at[:, :, 1 - c], cores[n].at[token],
-                rs1_send.at[token, n], rs1_recv.at[token, n], me, d_c,
-            )
-            for n in range(3)
-        ]
-
-    def rs2(token):
+    def rs1(token, n):
+        return remote(
+            parts[n].at[:, :, 1 - c], cores[n].at[token],
+            rs1_send.at[token, n], rs1_recv.at[token, n], me, d_c,
+        )
+
+    def rs2(token, n):
         return [
             remote(
                 cores[n].at[token, :, (y + dy) % 4], over_y[n].at[token, dy - 1],
@@ -239,17 +242,13 @@
                 me, dp_of(xh, (y + dy) % 4, c),
             )
             for dy in (1, 2, 3)
-            for n in range(3)
         ]
 
-    def rs3(token):
-        return [
-            remote(
-                sums[n].at[token], over_x[n].at[token],
-                rs3_send.at[token, n], rs3_recv.at[token, n], me, d_x,
-            )
-            for n in range(3)
-        ]
+    def rs3(token, n):
+        return remote(
+            sums[n].at[token], over_x[n].at[token],
+            rs3_send.at[token, n], rs3_recv.at[token, n], me, d_x,
+        )
 
     def outgoing(token, i):
         return remote(
@@ -290,23 +289,26 @@
 
         lax.fori_loop(0, samples // BLOCK, step, 0)
 
-    def weight_terms(token):
+    def weight_term(n, token):
+        if n == 2:
+            cut = hid.shape[1] // 2
+
+            def step_down(i, _):
+                left = hid[:, pl.ds(pl.multiple_of(i * cut, LANES), cut)]
+                p_down[i] = tn(left, mixed[token, 1]).astype(BF).reshape(p_down.shape[1:])
+                return 0
+
+            lax.fori_loop(0, 2, step_down, 0)
+            return
+        part, right = ((p_gate, g_gate), (p_up, g_up))[n]
+
         def step(i, _):
             left = mixed[token, 0, :, pl.ds(pl.multiple_of(i * BLOCK, BLOCK), BLOCK)]
             at = pl.ds((i % 2) * 2, 2)
-            p_gate[i // 2, at] = tn(left, g_gate[...]).astype(BF).reshape(2, 2, *p_gate.shape[3:])
-            p_up[i // 2, at] = tn(left, g_up[...]).astype(BF).reshape(2, 2, *p_up.shape[3:])
+            part[i // 2, at] = tn(left, right[...]).astype(BF).reshape(2, 2, *part.shape[3:])
             return 0
 
         lax.fori_loop(0, 4, step, 0)
-        cut = hid.shape[1] // 2
-
-        def step_down(i, _):
-            left = hid[:, pl.ds(pl.multiple_of(i * cut, LANES), cut)]
-            p_down[i] = tn(left, mixed[token, 1]).astype(BF).reshape(p_down.shape[1:])
-            return 0
-
-        lax.fori_loop(0, 2, step_down, 0)
 
     def backward(token):
         def step(i, _):
@@ -318,15 +320,17 @@
 
         lax.fori_loop(0, samples // BLOCK, step, 0)
 
-    def core_sum(token):
+    def core_stage(token, n):
+        rs1(token, n).wait_recv()
+
         def step(k, _):
             a, b = k // 4, k % 4
-            for n in range(3):
-                total = parts[n][a, b, c].astype(F32) + cores[n][token, a, b].astype(F32)
-                cores[n][token, a, b] = total.astype(BF)
+            total = parts[n][a, b, c].astype(F32) + cores[n][token, a, b].astype(F32)
+            cores[n][token, a, b] = total.astype(BF)
             return 0
 
         lax.fori_loop(0, 8, step, 0)
+        start_all(rs2(token, n))
 
     def y_sum(n, token, at):
         total = cores[n][token, at, y].astype(F32)
@@ -334,30 +338,32 @@
             total = total + over_y[n][token, dy, at].astype(F32)
         return total
 
-    def y_stage(token):
-        for copy in rs2(token):
+    def y_stage(token, n):
+        for copy in rs2(token, n):
             copy.wait()
-        for n in range(3):
-            sums[n][token] = y_sum(n, token, 1 - xh).astype(BF)
-
-    def x_stage(token):
-        for copy in rs3(token):
-            copy.wait()
-        for n in range(3):
-            total = y_sum(n, token, xh) + over_x[n][token].astype(F32)
-            results[n][token] = (total * factor).astype(BF)
+        sums[n][token] = y_sum(n, token, 1 - xh).astype(BF)
+        rs3(token, n).start()
+
+    def x_stage(token, n):
+        rs3(token, n).wait()
+        total = y_sum(n, token, xh) + over_x[n][token].astype(F32)
+        results[n][token] = (total * factor).astype(BF)
 
     def compute(token):
         forward(token)
         if token == 1:
-            for copy in first_terms:
-                copy.wait_send()
-            y_stage(0)
-            start_all(rs3(0))
-        weight_terms(token)
+            for n in (2, 0, 1):
+                rs1(0, n).wait_send()
+                y_stage(0, n)
+        weight_term(2, token)
+        rs1(token, 2).start()
+        weight_term(0, token)
+        rs1(token, 0).start()
+        core_stage(token, 2)
+        weight_term(1, token)
+        rs1(token, 1).start()
+        core_stage(token, 0)
         backward(token)
-        terms = rs1(token)
-        start_all(terms)
 
         def send_back(i, _):
             outgoing(token, i).start()
@@ -365,17 +371,12 @@
 
         lax.fori_loop(1, TOKEN_DEVICES, send_back, 0)
         own_back(token).start()
-        for copy in terms:
-            copy.wait_recv()
-        core_sum(token)
-        start_all(rs2(token))
-        return terms
+        core_stage(token, 1)
 
     wait_in(0)
-    first_terms = compute(0)
+    compute(0)
     wait_in(1)
-    second_terms = compute(1)
-    x_stage(0)
+    compute(1)
 
     def write(i):
         return pltpu.make_async_copy(
@@ -388,36 +389,42 @@
         target = x_raw.at[i].reshape(2 * samples, LANES)
 
         def step(k, _):
-            row = pl.multiple_of(k * ROWS, ROWS)
-            even, odd = halves(
-                back[0, q, pl.ds(row, ROWS), :].astype(F32), back[1, q, pl.ds(row, ROWS), :].astype(F32)
-            )
-            tmp[pl.ds(0, ROWS, stride=2), :] = even
-            tmp[pl.ds(1, ROWS, stride=2), :] = odd
-            both = pl.ds(2 * row, 2 * ROWS)
-            target[both, :] = (tmp[...] + cot[both, :].astype(F32)).astype(BF)
-            return 0
-
-        lax.fori_loop(0, samples // ROWS, step, 0)
+            rows = [pl.multiple_of((k * UNROLL + u) * ROWS, ROWS) for u in range(UNROLL)]
+            for u, row in enumerate(rows):
+                at = pl.ds(row, ROWS)
+                even, odd = halves(back[0, q, at, :].astype(F32), back[1, q, at, :].astype(F32))
+                tmp[u, pl.ds(0, ROWS, stride=2), :] = even
+                tmp[u, pl.ds(1, ROWS, stride=2), :] = odd
+            for u, row in enumerate(rows):
+                both = pl.ds(2 * row, 2 * ROWS)
+                target[both, :] = (tmp[u] + cot[both, :].astype(F32)).astype(BF)
+            return 0
+
+        lax.fori_loop(0, samples // (ROWS * UNROLL), step, 0)
         write(i).start()
+
+    def take_back(i):
+        outgoing(0, inverse(i)).wait_recv()
+        outgoing(1, inverse(i)).wait_recv()
+        finish(i)
 
     own_back(0).wait()
     own_back(1).wait()
     finish(0)
-
-    def take_back(i, _):
-        outgoing(0, inverse(i)).wait_recv()
-        outgoing(1, inverse(i)).wait_recv()
-        finish(i)
-        return 0
-
-    lax.fori_loop(1, 5, take_back, 0)
-    y_stage(1)
-    start_all(rs3(1))
-    lax.fori_loop(5, TOKEN_DEVICES, take_back, 0)
-    x_stage(1)
-    for copy in second_terms:
-        copy.wait_send()
+    y_stage(1, 2)
+    for n in range(3):
+        x_stage(0, n)
+    for i in (2, 4, 6):
+        take_back(i)
+    y_stage(1, 0)
+    take_back(1)
+    y_stage(1, 1)
+    for i in (7, 5, 3):
+        take_back(i)
+    for n in (2, 0, 1):
+        x_stage(1, n)
+    for n in range(3):
+        rs1(1, n).wait_send()
 
     def drain(i, _):
         outgoing(0, i).wait_send()
@@ -427,6 +434,26 @@
 
     lax.fori_loop(1, TOKEN_DEVICES, drain, 0)
     write(0).wait()
+
+
+def deliver(*refs):
+    sources, targets, held = refs[:4], refs[4:8], refs[8:12]
+    in_sem, out_sem = refs[12:]
+    rows = sources[0].shape[0] // PIECES
+    routes = [
+        tuple(ref.at[pl.ds(k * rows, rows)] for ref in (sources[0], held[0], targets[0]))
+        for k in range(PIECES)
+    ]
+    routes += [(sources[n], held[n], targets[n]) for n in (1, 2, 3)]
+    takes = [pltpu.make_async_copy(a, b, in_sem.at[k]) for k, (a, b, _) in enumerate(routes)]
+    gives = [pltpu.make_async_copy(b, o, out_sem.at[k]) for k, (_, b, o) in enumerate(routes)]
+    for take in takes:
+        take.start()
+    for take, give in zip(takes, gives, strict=True):
+        take.wait()
+        give.start()
+    for give in gives:
+        give.wait()
 
 
 def solution(mesh):
@@ -448,7 +475,7 @@
 
         raw = pltpu.VMEM((TOKEN_DEVICES, samples, owned, LANES), BF)
         hidden = pltpu.VMEM((samples, ff), BF)
-        return pl.pallas_call(
+        made = pl.pallas_call(
             functools.partial(kernel, factor),
             name="mixer_backward",
             out_shape=(
@@ -465,7 +492,7 @@
                 pltpu.VMEM((2, 2, samples, width), BF),
                 *three(2, DP),
                 hidden, hidden, hidden,
-                pltpu.VMEM((2 * ROWS, LANES), F32),
+                pltpu.VMEM((UNROLL, 2 * ROWS, LANES), F32),
                 *three(2, 4, 2),
                 *three(2, 2, 4),
                 *three(2, 3, 2),
@@ -482,6 +509,20 @@
                 collective_id=0, has_side_effects=True, vmem_limit_bytes=67_000_000
             ),
         )(inputs, cotangent, w_gate, w_up, w_down)
+        shapes = tuple(jax.ShapeDtypeStruct(a.shape, a.dtype) for a in made)
+        return pl.pallas_call(
+            deliver,
+            name="deliver",
+            out_shape=shapes,
+            in_specs=[anywhere] * 4,
+            out_specs=(anywhere,) * 4,
+            scratch_shapes=[
+                *(pltpu.VMEM(a.shape, a.dtype) for a in made),
+                dma((PIECES + 3,)),
+                dma((PIECES + 3,)),
+            ],
+            compiler_params=pltpu.CompilerParams(vmem_limit_bytes=67_000_000),
+        )(*made)
 
     return jax.shard_map(
         per_device,

time: 188 us -> 178 us (0.947)
  local copies, waits for them, and re-layouts: 9.18 us -> 0 us
    unnamed x10 -> x0, local copies, waits for them, and re-layouts: 9.18 us -> none
    pallas_call x1, Pallas kernels: 178 us -> 173 us  [per_device(): pl.pallas_call(functools.partial(kernel, factor), name='mixer_backward',...]
    pallas_call x0 -> x1, Pallas kernels: none -> 3.61 us  [per_device(): pl.pallas_call(deliver, name='deliver', out_shape=shapes, in_specs=[anywh...]
where the time goes in v2:
time: 178 us
  Pallas kernels  177 us (99%)
    pallas_call x1, Pallas kernels, per_device(): pl.pallas_call(functools.partial(kernel, factor), name='mixer_backward',...  173 us
    pallas_call x1, Pallas kernels, per_device(): pl.pallas_call(deliver, name='deliver', out_shape=shapes, in_specs=[anywh...  3.61 us

profile of v2, /device:TPU:0, one launch (start us, length us, event | category | flops | bytes accessed | tf_op | source)
XLA Modules:
  0.0 177.6 jit_solution(18195531247676340217)
XLA Ops:
  0.6 173.3 %mixer_backward.1 = (bf16[1024,2,1024]{2,1,0:T(2,128)(2,1)}, bf16[2,64,768]{2,1,0:T(8,128)(2,1)}, bf16[2,64,768]{2,1,0:T(8,128)(2,1)}, bf16[2,48,1024]{2,1,0:T(8,128)(2,1)}) custom-call(bf16[1024,2,1024]{2,1,0:T(2,128)(2,1)} %x.1, bf16[1024,2,1024]{2,1,0:T(2,128)(2,1)} %g.1, bf16[2,64,768]{2,1,0:T(8,128)(2,1)} %w_gate.1, bf16[2,64,768]{2,1,0:T(8,128)(2,1)} %w_up.1, ...), custom_call_target="tpu_custom_call" | custom-call | tf_op jit(solution)/shard_map/mixer_backward/pallas_call | solution.py:478
  174.0 3.6 %deliver.1 = (bf16[1024,2,1024]{2,1,0:T(2,128)(2,1)}, bf16[2,64,768]{2,1,0:T(8,128)(2,1)}, bf16[2,64,768]{2,1,0:T(8,128)(2,1)}, bf16[2,48,1024]{2,1,0:T(8,128)(2,1)}) custom-call(bf16[1024,2,1024]{2,1,0:T(2,128)(2,1)} %get-tuple-element.8.refs_0_, bf16[2,64,768]{2,1,0:T(8,128)(2,1)} %get-tuple-element.9.refs_1_, ...), custom_call_target="tpu_custom_call" | custom-call | tf_op jit(solution)/shard_map/deliver/pallas_call | solution.py:513

commit v3 on v2

--- a/solution.py
+++ b/solution.py
@@ -49,6 +49,8 @@
     y_gate, y_up, y_down,
     s_gate, s_up, s_down,
     r_gate, r_up, r_down,
+    v_gate, v_up, v_down,
+    u_gate, u_up, u_down,
     back,
     load_sem, own_sem, wload_sem, in_send, in_recv, out_send, out_recv, own_out_sem, write_sem,
     ag_send, ag_recv, rs1_send, rs1_recv, rs2_send, rs2_recv, rs3_send, rs3_recv,
@@ -62,8 +64,16 @@
     def dp_of(xh_, y_, c_):
         return xh_ * 8 + y_ * 2 + c_
 
+    inner = z * 2 + 1 - xl
+    mate = (inner, dp_of(1 - xh, y, c))
+    first, second = dp_of(0, y, c), dp_of(1, y, c)
+    computed = z * 2 + (xl + xh) % 2
+
     def partner(i):
         return ((z + i // 2) % 4) * 2 + (xl + i % 2) % 2
+
+    def partner_computes(i):
+        return ((z + i // 2) % 4) * 2 + (xl + xh + i % 2) % 2
 
     def inverse(i):
         return ((4 - i // 2) % 4) * 2 + i % 2
@@ -80,7 +90,7 @@
     def load(i, which):
         src, dst = ((x, x_raw), (g, g_raw))[which]
         return pltpu.make_async_copy(
-            src.at[:, :, columns(partner(i))], dst.at[i], load_sem.at[which, i]
+            src.at[:, :, columns(partner_computes(i))], dst.at[i], load_sem.at[which, i]
         )
 
     def start_loads(i, _):
@@ -96,8 +106,11 @@
             ((w_gate, full_gate), (w_up, full_up), (w_down, full_down))
         )
     ]
-    for copy in own_weights:
-        copy.start()
+
+    @pl.when(xh == 0)
+    def _():
+        for copy in own_weights:
+            copy.start()
 
     barrier = pltpu.get_barrier_semaphore()
 
@@ -110,42 +123,95 @@
         dp_of(xh, (y + 1) % 4, c),
         dp_of(xh, (y + 2) % 4, c),
         dp_of(xh, (y + 3) % 4, c),
-        dp_of(1 - xh, y, c),
         dp_of(xh, y, 1 - c),
     ):
         pl.semaphore_signal(barrier, inc=1, device_id=(me, to), device_id_type=MESH)
+    pl.semaphore_signal(barrier, inc=1, device_id=mate, device_id_type=MESH)
     pl.semaphore_wait(barrier, 12)
 
     fulls = (full_gate, full_up, full_down)
     mine = (w_gate, w_up, w_down)
-    d_x = dp_of(1 - xh, y, c)
+    relays = (v_gate, v_up, v_down)
+    passing = (u_gate, u_up, u_down)
     d_c = dp_of(xh, y, 1 - c)
 
-    def gather(slot, shard, to, srcs=None):
+    def gather(token, slot, shard, to, srcs=None, dsts=None):
         return [
             remote(
-                (srcs[n] if srcs else fulls[n].at[:, shard]), fulls[n].at[:, shard],
-                ag_send.at[slot, n], ag_recv.at[slot, n], me, to,
+                srcs[n] if srcs else fulls[n].at[token, shard],
+                dsts[n] if dsts else fulls[n].at[token, shard],
+                ag_send.at[token, slot, n], ag_recv.at[token, slot, n], *to,
             )
             for n in range(3)
         ]
 
-    ag_own_x = gather(0, d, d_x, mine)
-    ag_own_y = [gather(dy, d, dp_of(xh, (y + dy) % 4, c), mine) for dy in (1, 2, 3)]
-    ag_own_c = gather(4, d, d_c, mine)
-    ag_far_y = [gather(4 + dy, d_x, dp_of(xh, (y + dy) % 4, c)) for dy in (1, 2, 3)]
-    ag_far_c = gather(8, d_x, d_c)
-    ag_pass_own = [gather(8 + dy, dp_of(xh, (y + 4 - dy) % 4, c), d_c) for dy in (1, 2, 3)]
-    ag_pass_far = [gather(11 + dy, dp_of(1 - xh, (y + 4 - dy) % 4, c), d_c) for dy in (1, 2, 3)]
+    own = [[ref.at[token] for ref in mine] for token in range(2)]
+    other_core = (me, d_c)
+    first_x = [gather(token, 0, first, mate) for token in range(2)]
+    second_x = (
+        gather(0, 1, second, (inner, d), own[0]),
+        gather(1, 1, second, (inner, d), relays),
+    )
+    second_mate = [gather(token, 2, second, mate) for token in range(2)]
+    relay_x = gather(1, 3, second, mate, own[1], relays)
+
+    def over_y_copies(token, far):
+        shard = (first, second)[far]
+        return [
+            gather(token, 3 + 3 * far + dy, shard, (me, dp_of(xh, (y + dy) % 4, c))) for dy in (1, 2, 3)
+        ]
+
+    def core_copies(token, far):
+        return gather(token, 10 + far, (first, second)[far], other_core)
+
+    def pass_copies(token, far):
+        return [
+            gather(token, 11 + 3 * far + dy, dp_of(far, (y + 4 - dy) % 4, c), other_core)
+            for dy in (1, 2, 3)
+        ]
 
     def start_all(copies):
         for copy in copies:
             copy.start()
 
-    start_all(ag_own_x)
-    for copies in ag_own_y:
-        start_all(copies)
-    start_all(ag_own_c)
+    def recv_all(copies):
+        for copy in copies:
+            copy.wait_recv()
+
+    def send_all(copies):
+        for copy in copies:
+            copy.wait_send()
+
+    def spread(token, far):
+        for copies in over_y_copies(token, far):
+            start_all(copies)
+        start_all(core_copies(token, far))
+
+    def pass_on(token, far):
+        for arrived, onward in zip(
+            over_y_copies(token, far), pass_copies(token, far), strict=True
+        ):
+            recv_all(arrived)
+            start_all(onward)
+
+    def gathered(token):
+        for far in range(2):
+            recv_all(core_copies(token, far))
+            for copies in pass_copies(token, far):
+                recv_all(copies)
+
+    @pl.when(xh == 0)
+    def _():
+        for copy in own_weights:
+            copy.wait()
+        start_all(first_x[0])
+        spread(0, 0)
+        start_all(first_x[1])
+
+    @pl.when(xh == 1)
+    def _():
+        start_all(second_x[0])
+        start_all(relay_x)
 
     def incoming(token, which, i):
         return remote(
@@ -171,20 +237,39 @@
 
         lax.fori_loop(0, samples // (ROWS * UNROLL), step, 0)
 
-    def send_in(i, _):
+    def order(k):
+        return jnp.where(k < 2, 1 + 2 * k, jnp.where(k < 5, 2 * k - 2, 2 * k - 5))
+
+    def send_in(k, _):
+        i = order(k)
         shuffle(i, 0)
 
-        @pl.when(i > 1)
+        @pl.when(k > 0)
         def _():
-            incoming(0, 1, i - 1).start()
+            incoming(0, 1, order(k - 1)).start()
 
         shuffle(i, 1)
         incoming(0, 0, i).start()
         return 0
 
-    lax.fori_loop(1, TOKEN_DEVICES, send_in, 0)
+    lax.fori_loop(0, 5, send_in, 0)
+
+    @pl.when(xh == 0)
+    def _():
+        recv_all(relay_x)
+        start_all(second_x[1])
+
+    @pl.when(xh == 1)
+    def _():
+        recv_all(first_x[0])
+        spread(0, 0)
+        recv_all(second_x[0])
+        start_all(second_mate[0])
+        spread(0, 1)
+
+    lax.fori_loop(5, 7, send_in, 0)
     shuffle(0, 0)
-    incoming(0, 1, TOKEN_DEVICES - 1).start()
+    incoming(0, 1, order(6)).start()
     shuffle(0, 1)
 
     def send_in_b(i, _):
@@ -202,23 +287,34 @@
     ]
     start_all(own_in)
 
-    for copy in ag_own_x:
-        copy.wait()
-    for copies in ag_far_y:
-        start_all(copies)
-    start_all(ag_far_c)
-    for n in range(3):
-        for copy in ag_own_y[n]:
-            copy.wait()
-        start_all(ag_pass_own[n])
-    for n in range(3):
-        for copy in ag_far_y[n]:
-            copy.wait()
-        start_all(ag_pass_far[n])
-    for copies in (ag_own_c, ag_far_c, *ag_pass_own, *ag_pass_far):
-        for copy in copies:
-            copy.wait()
-    for copy in (*own_weights, *own_in):
+    @pl.when(xh == 0)
+    def _():
+        recv_all(second_mate[0])
+        spread(0, 1)
+
+    @pl.when(xh == 1)
+    def _():
+        recv_all(first_x[1])
+
+    spread(1, 0)
+    pass_on(0, 0)
+
+    @pl.when(xh == 0)
+    def _():
+        recv_all(second_x[1])
+        start_all(second_mate[1])
+        spread(1, 1)
+
+    pass_on(0, 1)
+
+    @pl.when(xh == 1)
+    def _():
+        recv_all(second_mate[1])
+        spread(1, 1)
+
+    pass_on(1, 0)
+    gathered(0)
+    for copy in own_in:
         copy.wait()
 
     parts = (p_gate, p_up, p_down)
@@ -244,21 +340,36 @@
             for dy in (1, 2, 3)
         ]
 
-    def rs3(token, n):
+    def rs3(token, n, slot):
         return remote(
-            sums[n].at[token], over_x[n].at[token],
-            rs3_send.at[token, n], rs3_recv.at[token, n], me, d_x,
+            sums[n].at[token, slot], over_x[n].at[token, slot],
+            rs3_send.at[token, n, slot], rs3_recv.at[token, n, slot], *mate,
+        )
+
+    def rs_relay(n):
+        return remote(
+            sums[n].at[0, 0], passing[n], rs3_send.at[0, n, 2], rs3_recv.at[0, n, 2], inner, d
+        )
+
+    def rs_relayed(n):
+        return remote(
+            passing[n], over_x[n].at[0, 0], rs3_send.at[0, n, 0], rs3_recv.at[0, n, 0], *mate
+        )
+
+    def rs_last(n):
+        return remote(
+            sums[n].at[1, 1], over_x[n].at[1, 1], rs3_send.at[1, n, 1], rs3_recv.at[1, n, 1], inner, d
         )
 
     def outgoing(token, i):
         return remote(
-            stage.at[token, 0, partner(i)], back.at[token, me],
+            stage.at[token, 0, partner(i)], back.at[token, computed],
             out_send.at[token, i], out_recv.at[token, i], partner(i), d,
         )
 
     def own_back(token):
         return pltpu.make_async_copy(
-            stage.at[token, 0, me], back.at[token, me], own_out_sem.at[token]
+            stage.at[token, 0, me], back.at[token, computed], own_out_sem.at[token]
         )
 
     def wait_in(token):
@@ -338,23 +449,66 @@
             total = total + over_y[n][token, dy, at].astype(F32)
         return total
 
+    def emit(n, token, total):
+        results[n][token] = (total * factor).astype(BF)
+
     def y_stage(token, n):
         for copy in rs2(token, n):
             copy.wait()
-        sums[n][token] = y_sum(n, token, 1 - xh).astype(BF)
-        rs3(token, n).start()
+        if token == 0:
+
+            @pl.when(xh == 1)
+            def _():
+                for slot in range(2):
+                    sums[n][0, slot] = y_sum(n, 0, slot).astype(BF)
+                    rs3(0, n, slot).start()
+        else:
+            sums[n][1, 0] = y_sum(n, 1, 1 - xh).astype(BF)
+            rs3(1, n, 0).start()
 
     def x_stage(token, n):
-        rs3(token, n).wait()
-        total = y_sum(n, token, xh) + over_x[n][token].astype(F32)
-        results[n][token] = (total * factor).astype(BF)
+        if token == 0:
+
+            @pl.when(xh == 0)
+            def _():
+                rs3(0, n, 0).wait_recv()
+                rs3(0, n, 1).wait_recv()
+                sums[n][0, 0] = (y_sum(n, 0, 1) + over_x[n][0, 1].astype(F32)).astype(BF)
+                rs_relay(n).start()
+                emit(n, 0, y_sum(n, 0, 0) + over_x[n][0, 0].astype(F32))
+        else:
+            rs3(1, n, 0).wait()
+            total = y_sum(n, 1, xh) + over_x[n][1, 0].astype(F32)
+
+            @pl.when(xh == 0)
+            def _():
+                emit(n, 1, total)
+
+            @pl.when(xh == 1)
+            def _():
+                sums[n][1, 1] = total.astype(BF)
+                rs_last(n).start()
+
+    def relay_stage(n):
+        @pl.when(xh == 0)
+        def _():
+            rs_relay(n).wait_recv()
+            rs_relayed(n).start()
+
+    def last_stage(token, n):
+        @pl.when(xh == 1)
+        def _():
+            (rs_relayed(n) if token == 0 else rs_last(n)).wait_recv()
+            emit(n, token, over_x[n][token, token].astype(F32))
 
     def compute(token):
         forward(token)
         if token == 1:
-            for n in (2, 0, 1):
+            y_stage(0, 1)
+            x_stage(0, 2)
+            x_stage(0, 0)
+            for n in range(3):
                 rs1(0, n).wait_send()
-                y_stage(0, n)
         weight_term(2, token)
         rs1(token, 2).start()
         weight_term(0, token)
@@ -364,6 +518,8 @@
         rs1(token, 1).start()
         core_stage(token, 0)
         backward(token)
+        if token == 1:
+            x_stage(0, 1)
 
         def send_back(i, _):
             outgoing(token, i).start()
@@ -375,16 +531,20 @@
 
     wait_in(0)
     compute(0)
+    pass_on(1, 1)
+    gathered(1)
+    y_stage(0, 2)
+    y_stage(0, 0)
     wait_in(1)
     compute(1)
 
     def write(i):
         return pltpu.make_async_copy(
-            x_raw.at[i], out.at[:, :, columns(partner(i))], write_sem.at[i]
+            x_raw.at[i], out.at[:, :, columns(partner_computes(i))], write_sem.at[i]
         )
 
     def finish(i):
-        q = partner(i)
+        q = partner_computes(i)
         cot = g_raw.at[i].reshape(2 * samples, LANES)
         target = x_raw.at[i].reshape(2 * samples, LANES)
 
@@ -411,20 +571,52 @@
     own_back(0).wait()
     own_back(1).wait()
     finish(0)
+    for n in (2, 0, 1):
+        relay_stage(n)
     y_stage(1, 2)
-    for n in range(3):
-        x_stage(0, n)
     for i in (2, 4, 6):
         take_back(i)
     y_stage(1, 0)
+    x_stage(1, 2)
     take_back(1)
     y_stage(1, 1)
-    for i in (7, 5, 3):
-        take_back(i)
+    x_stage(1, 0)
+    take_back(7)
+    x_stage(1, 1)
+    take_back(5)
     for n in (2, 0, 1):
-        x_stage(1, n)
+        last_stage(0, n)
+    take_back(3)
+    for n in (2, 0, 1):
+        last_stage(1, n)
+
+    for token in range(2):
+        for far in range(2):
+            for copies in (*over_y_copies(token, far), *pass_copies(token, far)):
+                send_all(copies)
+            send_all(core_copies(token, far))
     for n in range(3):
         rs1(1, n).wait_send()
+
+    @pl.when(xh == 0)
+    def _():
+        send_all(first_x[0])
+        send_all(first_x[1])
+        send_all(second_x[1])
+        send_all(second_mate[1])
+        for n in range(3):
+            rs_relay(n).wait_send()
+            rs_relayed(n).wait_send()
+
+    @pl.when(xh == 1)
+    def _():
+        send_all(second_x[0])
+        send_all(second_mate[0])
+        send_all(relay_x)
+        for n in range(3):
+            rs3(0, n, 0).wait_send()
+            rs3(0, n, 1).wait_send()
+            rs_last(n).wait_send()
 
     def drain(i, _):
         outgoing(0, i).wait_send()
@@ -496,14 +688,16 @@
                 *three(2, 4, 2),
                 *three(2, 2, 4),
                 *three(2, 3, 2),
-                *three(2),
-                *three(2),
+                *three(2, 2),
+                *three(2, 2),
+                *three(),
+                *three(),
                 pltpu.VMEM((2, TOKEN_DEVICES, samples, LANES), BF),
                 dma((2, TOKEN_DEVICES)), dma((2, 2)), dma((3,)),
                 dma((2, 2, TOKEN_DEVICES)), dma((2, 2, TOKEN_DEVICES)),
                 dma((2, TOKEN_DEVICES)), dma((2, TOKEN_DEVICES)), dma((2,)), dma((TOKEN_DEVICES,)),
-                dma((15, 3)), dma((15, 3)),
-                dma((2, 3)), dma((2, 3)), dma((2, 3, 3)), dma((2, 3, 3)), dma((2, 3)), dma((2, 3)),
+                dma((2, 18, 3)), dma((2, 18, 3)),
+                dma((2, 3)), dma((2, 3)), dma((2, 3, 3)), dma((2, 3, 3)), dma((2, 3, 3)), dma((2, 3, 3)),
             ],
             compiler_params=pltpu.CompilerParams(
                 collective_id=0, has_side_effects=True, vmem_limit_bytes=67_000_000

time: 178 us -> 170 us (0.955)
  Pallas kernels: 177 us -> 169 us
    pallas_call x1, Pallas kernels: 173 us -> 166 us  [per_device(): pl.pallas_call(functools.partial(kernel, factor), name='mixer_backward',...]
where the time goes in v3:
time: 170 us
  Pallas kernels  169 us (99%)
    pallas_call x1, Pallas kernels, per_device(): pl.pallas_call(functools.partial(kernel, factor), name='mixer_backward',...  166 us
    pallas_call x1, Pallas kernels, per_device(): pl.pallas_call(deliver, name='deliver', out_shape=shapes, in_specs=[anywh...  3.61 us

profile of v3, /device:TPU:0, one launch (start us, length us, event | category | flops | bytes accessed | tf_op | source)
XLA Modules:
  0.0 170.1 jit_solution(12400874951320132251)
XLA Ops:
  0.6 165.7 %mixer_backward.1 = (bf16[1024,2,1024]{2,1,0:T(2,128)(2,1)}, bf16[2,64,768]{2,1,0:T(8,128)(2,1)}, bf16[2,64,768]{2,1,0:T(8,128)(2,1)}, bf16[2,48,1024]{2,1,0:T(8,128)(2,1)}) custom-call(bf16[1024,2,1024]{2,1,0:T(2,128)(2,1)} %x.1, bf16[1024,2,1024]{2,1,0:T(2,128)(2,1)} %g.1, bf16[2,64,768]{2,1,0:T(8,128)(2,1)} %w_gate.1, bf16[2,64,768]{2,1,0:T(8,128)(2,1)} %w_up.1, ...), custom_call_target="tpu_custom_call" | custom-call | tf_op jit(solution)/shard_map/mixer_backward/pallas_call | solution.py:670
  166.4 3.6 %deliver.1 = (bf16[1024,2,1024]{2,1,0:T(2,128)(2,1)}, bf16[2,64,768]{2,1,0:T(8,128)(2,1)}, bf16[2,64,768]{2,1,0:T(8,128)(2,1)}, bf16[2,48,1024]{2,1,0:T(8,128)(2,1)}) custom-call(bf16[1024,2,1024]{2,1,0:T(2,128)(2,1)} %get-tuple-element.8.refs_0_, bf16[2,64,768]{2,1,0:T(8,128)(2,1)} %get-tuple-element.9.refs_1_, ...), custom_call_target="tpu_custom_call" | custom-call | tf_op jit(solution)/shard_map/deliver/pallas_call | solution.py:707

commit v4 on v3

--- a/solution.py
+++ b/solution.py
@@ -17,7 +17,6 @@
 ROWS = 128
 BLOCK = 256
 UNROLL = 4
-PIECES = 4
 
 
 def nn(a, b):
@@ -41,8 +40,8 @@
 def kernel(
     factor,
     x, g, w_gate, w_up, w_down,
-    out, out_gate, out_up, out_down,
-    x_raw, g_raw, stage, mixed, full_gate, full_up, full_down,
+    blocks, out_gate, out_up, out_down,
+    g_raw, stage, mixed, full_gate, full_up, full_down,
     hid, g_gate, g_up, tmp,
     p_gate, p_up, p_down,
     c_gate, c_up, c_down,
@@ -52,10 +51,18 @@
     v_gate, v_up, v_down,
     u_gate, u_up, u_down,
     back,
-    load_sem, own_sem, wload_sem, in_send, in_recv, out_send, out_recv, own_out_sem, write_sem,
+    load_sem, own_sem, wload_sem, in_send, in_recv, out_send, out_recv, own_out_sem,
     ag_send, ag_recv, rs1_send, rs1_recv, rs2_send, rs2_recv, rs3_send, rs3_recv,
 ):
     samples = x.shape[0]
+
+    def wait_for(ref, sem):
+        pltpu.make_async_copy(ref, ref, sem).wait()
+
+    def wait_shards(count, sem):
+        held = full_gate.at[0, pl.ds(0, count)] if count <= DP else full_gate.at[:, pl.ds(0, count // 2)]
+        wait_for(held, sem)
+
     me = lax.axis_index("token")
     z, xl = me // 2, me % 2
     d = lax.axis_index("dp")
@@ -88,10 +95,9 @@
         )
 
     def load(i, which):
-        src, dst = ((x, x_raw), (g, g_raw))[which]
-        return pltpu.make_async_copy(
-            src.at[:, :, columns(partner_computes(i))], dst.at[i], load_sem.at[which, i]
-        )
+        q = partner_computes(i)
+        src, dst = ((x, blocks.at[q]), (g, g_raw.at[i]))[which]
+        return pltpu.make_async_copy(src.at[:, :, columns(q)], dst, load_sem.at[i])
 
     def start_loads(i, _):
         load(i, 0).start()
@@ -101,10 +107,8 @@
     lax.fori_loop(1, TOKEN_DEVICES, start_loads, 0)
     start_loads(0, 0)
     own_weights = [
-        pltpu.make_async_copy(src, dst.at[:, d], wload_sem.at[n])
-        for n, (src, dst) in enumerate(
-            ((w_gate, full_gate), (w_up, full_up), (w_down, full_down))
-        )
+        pltpu.make_async_copy(src, dst.at[:, d], wload_sem)
+        for src, dst in ((w_gate, full_gate), (w_up, full_up), (w_down, full_down))
     ]
 
     @pl.when(xh == 0)
@@ -135,38 +139,38 @@
     passing = (u_gate, u_up, u_down)
     d_c = dp_of(xh, y, 1 - c)
 
-    def gather(token, slot, shard, to, srcs=None, dsts=None):
+    def gather(token, sends, recvs, shard, to, srcs=None, dsts=None):
         return [
             remote(
                 srcs[n] if srcs else fulls[n].at[token, shard],
                 dsts[n] if dsts else fulls[n].at[token, shard],
-                ag_send.at[token, slot, n], ag_recv.at[token, slot, n], *to,
+                ag_send.at[sends], ag_recv.at[recvs], *to,
             )
             for n in range(3)
         ]
 
     own = [[ref.at[token] for ref in mine] for token in range(2)]
     other_core = (me, d_c)
-    first_x = [gather(token, 0, first, mate) for token in range(2)]
+    first_x = [gather(token, 8 + token, 14 + token, first, mate) for token in range(2)]
     second_x = (
-        gather(0, 1, second, (inner, d), own[0]),
-        gather(1, 1, second, (inner, d), relays),
+        gather(0, 10, 16, second, (inner, d), own[0]),
+        gather(1, 11, 17, second, (inner, d), relays),
     )
-    second_mate = [gather(token, 2, second, mate) for token in range(2)]
-    relay_x = gather(1, 3, second, mate, own[1], relays)
+    second_mate = [gather(token, 12 + token, 18 + token, second, mate) for token in range(2)]
+    relay_x = gather(1, 14, 20, second, mate, own[1], relays)
 
     def over_y_copies(token, far):
-        shard = (first, second)[far]
+        shard, at = (first, second)[far], 2 * token + far
         return [
-            gather(token, 3 + 3 * far + dy, shard, (me, dp_of(xh, (y + dy) % 4, c))) for dy in (1, 2, 3)
+            gather(token, at, 3 * at + dy - 1, shard, (me, dp_of(xh, (y + dy) % 4, c))) for dy in (1, 2, 3)
         ]
 
     def core_copies(token, far):
-        return gather(token, 10 + far, (first, second)[far], other_core)
+        return gather(token, 2 * token + far, 12 + token, (first, second)[far], other_core)
 
     def pass_copies(token, far):
         return [
-            gather(token, 11 + 3 * far + dy, dp_of(far, (y + 4 - dy) % 4, c), other_core)
+            gather(token, 4 + 2 * token + far, 12 + token, dp_of(far, (y + 4 - dy) % 4, c), other_core)
             for dy in (1, 2, 3)
         ]
 
@@ -174,13 +178,8 @@
         for copy in copies:
             copy.start()
 
-    def recv_all(copies):
-        for copy in copies:
-            copy.wait_recv()
-
-    def send_all(copies):
-        for copy in copies:
-            copy.wait_send()
+    def arrived(slot):
+        wait_shards(3, ag_recv.at[slot])
 
     def spread(token, far):
         for copies in over_y_copies(token, far):
@@ -188,22 +187,16 @@
         start_all(core_copies(token, far))
 
     def pass_on(token, far):
-        for arrived, onward in zip(
-            over_y_copies(token, far), pass_copies(token, far), strict=True
-        ):
-            recv_all(arrived)
+        for k, onward in enumerate(pass_copies(token, far)):
+            arrived(3 * (2 * token + far) + k)
             start_all(onward)
 
     def gathered(token):
-        for far in range(2):
-            recv_all(core_copies(token, far))
-            for copies in pass_copies(token, far):
-                recv_all(copies)
+        wait_shards(24, ag_recv.at[12 + token])
 
     @pl.when(xh == 0)
     def _():
-        for copy in own_weights:
-            copy.wait()
+        wait_shards(6, wload_sem)
         start_all(first_x[0])
         spread(0, 0)
         start_all(first_x[1])
@@ -216,12 +209,13 @@
     def incoming(token, which, i):
         return remote(
             stage.at[token, which, i], mixed.at[token, which, :, columns(me)],
-            in_send.at[token, which, i], in_recv.at[token, which, i], partner(i), d,
+            in_send.at[token], in_recv.at[token], partner(i), d,
         )
 
     def shuffle(i, which):
-        load(i, which).wait()
-        raw = ((x_raw, g_raw)[which]).at[i].reshape(2 * samples, LANES)
+        if which == 0:
+            wait_for(g_raw.at[pl.ds(0, 2)], load_sem.at[i])
+        raw = (blocks.at[partner_computes(i)], g_raw.at[i])[which].reshape(2 * samples, LANES)
 
         def step(k, _):
             rows = [pl.multiple_of((k * UNROLL + u) * ROWS, ROWS) for u in range(UNROLL)]
@@ -256,14 +250,14 @@
 
     @pl.when(xh == 0)
     def _():
-        recv_all(relay_x)
+        arrived(20)
         start_all(second_x[1])
 
     @pl.when(xh == 1)
     def _():
-        recv_all(first_x[0])
+        arrived(14)
         spread(0, 0)
-        recv_all(second_x[0])
+        arrived(16)
         start_all(second_mate[0])
         spread(0, 1)
 
@@ -280,7 +274,7 @@
     lax.fori_loop(1, TOKEN_DEVICES, send_in_b, 0)
     own_in = [
         pltpu.make_async_copy(
-            stage.at[token, which, 0], mixed.at[token, which, :, columns(me)], own_sem.at[token, which]
+            stage.at[token, which, 0], mixed.at[token, which, :, columns(me)], own_sem
         )
         for token in range(2)
         for which in range(2)
@@ -289,19 +283,19 @@
 
     @pl.when(xh == 0)
     def _():
-        recv_all(second_mate[0])
+        arrived(18)
         spread(0, 1)
 
     @pl.when(xh == 1)
     def _():
-        recv_all(first_x[1])
+        arrived(15)
 
     spread(1, 0)
     pass_on(0, 0)
 
     @pl.when(xh == 0)
     def _():
-        recv_all(second_x[1])
+        arrived(17)
         start_all(second_mate[1])
         spread(1, 1)
 
@@ -309,13 +303,12 @@
 
     @pl.when(xh == 1)
     def _():
-        recv_all(second_mate[1])
+        arrived(19)
         spread(1, 1)
 
     pass_on(1, 0)
     gathered(0)
-    for copy in own_in:
-        copy.wait()
+    wait_for(stage.at[:, :, 0], own_sem)
 
     parts = (p_gate, p_up, p_down)
     cores = (c_gate, c_up, c_down)
@@ -327,14 +320,14 @@
     def rs1(token, n):
         return remote(
             parts[n].at[:, :, 1 - c], cores[n].at[token],
-            rs1_send.at[token, n], rs1_recv.at[token, n], me, d_c,
+            rs1_send.at[token], rs1_recv.at[token, n], me, d_c,
         )
 
     def rs2(token, n):
         return [
             remote(
                 cores[n].at[token, :, (y + dy) % 4], over_y[n].at[token, dy - 1],
-                rs2_send.at[token, dy - 1, n], rs2_recv.at[token, dy - 1, n],
+                rs2_send.at[token], rs2_recv.at[token, n],
                 me, dp_of(xh, (y + dy) % 4, c),
             )
             for dy in (1, 2, 3)
@@ -343,42 +336,39 @@
     def rs3(token, n, slot):
         return remote(
             sums[n].at[token, slot], over_x[n].at[token, slot],
-            rs3_send.at[token, n, slot], rs3_recv.at[token, n, slot], *mate,
+            rs3_send.at[token], rs3_recv.at[6 * token + n], *mate,
         )
 
     def rs_relay(n):
         return remote(
-            sums[n].at[0, 0], passing[n], rs3_send.at[0, n, 2], rs3_recv.at[0, n, 2], inner, d
+            sums[n].at[0, 0], passing[n], rs3_send.at[0], rs3_recv.at[3 + n], inner, d
         )
 
     def rs_relayed(n):
         return remote(
-            passing[n], over_x[n].at[0, 0], rs3_send.at[0, n, 0], rs3_recv.at[0, n, 0], *mate
+            passing[n], over_x[n].at[0, 0], rs3_send.at[0], rs3_recv.at[n], *mate
         )
 
     def rs_last(n):
         return remote(
-            sums[n].at[1, 1], over_x[n].at[1, 1], rs3_send.at[1, n, 1], rs3_recv.at[1, n, 1], inner, d
+            sums[n].at[1, 1], over_x[n].at[1, 1], rs3_send.at[2], rs3_recv.at[9 + n], inner, d
         )
 
     def outgoing(token, i):
         return remote(
             stage.at[token, 0, partner(i)], back.at[token, computed],
-            out_send.at[token, i], out_recv.at[token, i], partner(i), d,
+            out_send.at[token], out_recv.at[i], partner(i), d,
         )
 
     def own_back(token):
         return pltpu.make_async_copy(
-            stage.at[token, 0, me], back.at[token, computed], own_out_sem.at[token]
+            stage.at[token, 0, me], back.at[token, computed], own_out_sem
         )
 
     def wait_in(token):
-        def body(i, _):
-            incoming(token, 0, i).wait()
-            incoming(token, 1, i).wait()
-            return 0
-
-        lax.fori_loop(1, TOKEN_DEVICES, body, 0)
+        sent = stage.at[token, :, pl.ds(1, TOKEN_DEVICES - 1)]
+        wait_for(sent, in_send.at[token])
+        wait_for(sent, in_recv.at[token])
 
     def weight(n, token):
         full = fulls[n]
@@ -432,7 +422,7 @@
         lax.fori_loop(0, samples // BLOCK, step, 0)
 
     def core_stage(token, n):
-        rs1(token, n).wait_recv()
+        wait_shards(8, rs1_recv.at[token, n])
 
         def step(k, _):
             a, b = k // 4, k % 4
@@ -453,8 +443,7 @@
         results[n][token] = (total * factor).astype(BF)
 
     def y_stage(token, n):
-        for copy in rs2(token, n):
-            copy.wait()
+        wait_shards(6, rs2_recv.at[token, n])
         if token == 0:
 
             @pl.when(xh == 1)
@@ -471,13 +460,12 @@
 
             @pl.when(xh == 0)
             def _():
-                rs3(0, n, 0).wait_recv()
-                rs3(0, n, 1).wait_recv()
+                wait_shards(2, rs3_recv.at[n])
                 sums[n][0, 0] = (y_sum(n, 0, 1) + over_x[n][0, 1].astype(F32)).astype(BF)
                 rs_relay(n).start()
                 emit(n, 0, y_sum(n, 0, 0) + over_x[n][0, 0].astype(F32))
         else:
-            rs3(1, n, 0).wait()
+            wait_shards(1, rs3_recv.at[6 + n])
             total = y_sum(n, 1, xh) + over_x[n][1, 0].astype(F32)
 
             @pl.when(xh == 0)
@@ -492,13 +480,13 @@
     def relay_stage(n):
         @pl.when(xh == 0)
         def _():
-            rs_relay(n).wait_recv()
+            wait_shards(1, rs3_recv.at[3 + n])
             rs_relayed(n).start()
 
     def last_stage(token, n):
         @pl.when(xh == 1)
         def _():
-            (rs_relayed(n) if token == 0 else rs_last(n)).wait_recv()
+            wait_shards(1, rs3_recv.at[9 * token + n])
             emit(n, token, over_x[n][token, token].astype(F32))
 
     def compute(token):
@@ -507,8 +495,7 @@
             y_stage(0, 1)
             x_stage(0, 2)
             x_stage(0, 0)
-            for n in range(3):
-                rs1(0, n).wait_send()
+            wait_shards(24, rs1_send.at[0])
         weight_term(2, token)
         rs1(token, 2).start()
         weight_term(0, token)
@@ -538,15 +525,10 @@
     wait_in(1)
     compute(1)
 
-    def write(i):
-        return pltpu.make_async_copy(
-            x_raw.at[i], out.at[:, :, columns(partner_computes(i))], write_sem.at[i]
-        )
-
     def finish(i):
         q = partner_computes(i)
         cot = g_raw.at[i].reshape(2 * samples, LANES)
-        target = x_raw.at[i].reshape(2 * samples, LANES)
+        target = blocks.at[q].reshape(2 * samples, LANES)
 
         def step(k, _):
             rows = [pl.multiple_of((k * UNROLL + u) * ROWS, ROWS) for u in range(UNROLL)]
@@ -561,15 +543,12 @@
             return 0
 
         lax.fori_loop(0, samples // (ROWS * UNROLL), step, 0)
-        write(i).start()
 
     def take_back(i):
-        outgoing(0, inverse(i)).wait_recv()
-        outgoing(1, inverse(i)).wait_recv()
+        wait_for(back.at[:, 0], out_recv.at[inverse(i)])
         finish(i)
 
-    own_back(0).wait()
-    own_back(1).wait()
+    wait_for(back.at[:, 0], own_out_sem)
     finish(0)
     for n in (2, 0, 1):
         relay_stage(n)
@@ -590,62 +569,41 @@
     for n in (2, 0, 1):
         last_stage(1, n)
 
+    for at in range(4):
+        wait_shards(12, ag_send.at[at])
+        wait_shards(9, ag_send.at[4 + at])
+    wait_shards(24, rs1_send.at[1])
     for token in range(2):
-        for far in range(2):
-            for copies in (*over_y_copies(token, far), *pass_copies(token, far)):
-                send_all(copies)
-            send_all(core_copies(token, far))
-    for n in range(3):
-        rs1(1, n).wait_send()
+        wait_shards(18, rs2_send.at[token])
+        wait_for(stage.at[token, 0, pl.ds(1, TOKEN_DEVICES - 1)], out_send.at[token])
+    wait_shards(6, rs3_send.at[0])
+    wait_shards(3, rs3_send.at[1])
 
     @pl.when(xh == 0)
     def _():
-        send_all(first_x[0])
-        send_all(first_x[1])
-        send_all(second_x[1])
-        send_all(second_mate[1])
-        for n in range(3):
-            rs_relay(n).wait_send()
-            rs_relayed(n).wait_send()
+        for at in (8, 9, 11, 13):
+            wait_shards(3, ag_send.at[at])
 
     @pl.when(xh == 1)
     def _():
-        send_all(second_x[0])
-        send_all(second_mate[0])
-        send_all(relay_x)
-        for n in range(3):
-            rs3(0, n, 0).wait_send()
-            rs3(0, n, 1).wait_send()
-            rs_last(n).wait_send()
-
-    def drain(i, _):
-        outgoing(0, i).wait_send()
-        outgoing(1, i).wait_send()
-        write(i).wait()
-        return 0
-
-    lax.fori_loop(1, TOKEN_DEVICES, drain, 0)
-    write(0).wait()
-
-
-def deliver(*refs):
-    sources, targets, held = refs[:4], refs[4:8], refs[8:12]
-    in_sem, out_sem = refs[12:]
-    rows = sources[0].shape[0] // PIECES
-    routes = [
-        tuple(ref.at[pl.ds(k * rows, rows)] for ref in (sources[0], held[0], targets[0]))
-        for k in range(PIECES)
+        for at in (10, 12, 14):
+            wait_shards(3, ag_send.at[at])
+        wait_shards(3, rs3_send.at[2])
+
+
+def deliver(blocks, gate, up, down, out, out_gate, out_up, out_down, sem):
+    copies = [
+        pltpu.make_async_copy(
+            blocks.at[q], out.at[:, :, pl.ds(q * LANES, LANES)], sem.at[q]
+        )
+        for q in range(TOKEN_DEVICES)
     ]
-    routes += [(sources[n], held[n], targets[n]) for n in (1, 2, 3)]
-    takes = [pltpu.make_async_copy(a, b, in_sem.at[k]) for k, (a, b, _) in enumerate(routes)]
-    gives = [pltpu.make_async_copy(b, o, out_sem.at[k]) for k, (_, b, o) in enumerate(routes)]
-    for take in takes:
-        take.start()
-    for take, give in zip(takes, gives, strict=True):
-        take.wait()
-        give.start()
-    for give in gives:
-        give.wait()
+    pairs = ((gate, out_gate), (up, out_up), (down, out_down))
+    copies += [pltpu.make_async_copy(a, b, sem.at[TOKEN_DEVICES + n]) for n, (a, b) in enumerate(pairs)]
+    for copy in copies:
+        copy.start()
+    for copy in copies:
+        copy.wait()
 
 
 def solution(mesh):
@@ -671,15 +629,15 @@
             functools.partial(kernel, factor),
             name="mixer_backward",
             out_shape=(
-                jax.ShapeDtypeStruct(inputs.shape, BF),
-                jax.ShapeDtypeStruct(w_gate.shape, BF),
-                jax.ShapeDtypeStruct(w_up.shape, BF),
-                jax.ShapeDtypeStruct(w_down.shape, BF),
+                raw,
+                pltpu.VMEM(w_gate.shape, BF),
+                pltpu.VMEM(w_up.shape, BF),
+                pltpu.VMEM(w_down.shape, BF),
             ),
             in_specs=[anywhere] * 5,
-            out_specs=(anywhere, vmem, vmem, vmem),
+            out_specs=(vmem,) * 4,
             scratch_shapes=[
-                raw, raw,
+                raw,
                 pltpu.VMEM((2, 2, TOKEN_DEVICES, samples, LANES), BF),
                 pltpu.VMEM((2, 2, samples, width), BF),
                 *three(2, DP),
@@ -693,30 +651,29 @@
                 *three(),
                 *three(),
                 pltpu.VMEM((2, TOKEN_DEVICES, samples, LANES), BF),
-                dma((2, TOKEN_DEVICES)), dma((2, 2)), dma((3,)),
-                dma((2, 2, TOKEN_DEVICES)), dma((2, 2, TOKEN_DEVICES)),
-                dma((2, TOKEN_DEVICES)), dma((2, TOKEN_DEVICES)), dma((2,)), dma((TOKEN_DEVICES,)),
-                dma((2, 18, 3)), dma((2, 18, 3)),
-                dma((2, 3)), dma((2, 3)), dma((2, 3, 3)), dma((2, 3, 3)), dma((2, 3, 3)), dma((2, 3, 3)),
+                dma((TOKEN_DEVICES,)), dma(()), dma(()),
+                dma((2,)), dma((2,)), dma((2,)), dma((TOKEN_DEVICES,)), dma(()),
+                dma((15,)), dma((21,)),
+                dma((2,)), dma((2, 3)), dma((2,)), dma((2, 3)), dma((3,)), dma((12,)),
             ],
             compiler_params=pltpu.CompilerParams(
-                collective_id=0, has_side_effects=True, vmem_limit_bytes=67_000_000
+                collective_id=0, has_side_effects=True, vmem_limit_bytes=62_000_000
             ),
         )(inputs, cotangent, w_gate, w_up, w_down)
-        shapes = tuple(jax.ShapeDtypeStruct(a.shape, a.dtype) for a in made)
         return pl.pallas_call(
             deliver,
             name="deliver",
-            out_shape=shapes,
-            in_specs=[anywhere] * 4,
+            out_shape=(
+                jax.ShapeDtypeStruct(inputs.shape, BF),
+                jax.ShapeDtypeStruct(w_gate.shape, BF),
+                jax.ShapeDtypeStruct(w_up.shape, BF),
+                jax.ShapeDtypeStruct(w_down.shape, BF),
+            ),
+            in_specs=[vmem] * 4,
             out_specs=(anywhere,) * 4,
-            scratch_shapes=[
-                *(pltpu.VMEM(a.shape, a.dtype) for a in made),
-                dma((PIECES + 3,)),
-                dma((PIECES + 3,)),
-            ],
-            compiler_params=pltpu.CompilerParams(vmem_limit_bytes=67_000_000),
-        )(*made)
+            scratch_shapes=[dma((TOKEN_DEVICES + 3,))],
+            compiler_params=pltpu.CompilerParams(vmem_limit_bytes=1_000_000),
+        )(*(pltpu.with_memory_space_constraint(a, pltpu.VMEM) for a in made))
 
     return jax.shard_map(
         per_device,

time: 170 us -> 164 us (0.965)
  Pallas kernels: 169 us -> 163 us
    pallas_call x1, Pallas kernels: 166 us -> 161 us  [per_device(): pl.pallas_call(functools.partial(kernel, factor), name='mixer_backward',...]
where the time goes in v4:
time: 164 us
  Pallas kernels  163 us (99%)
    pallas_call x1, Pallas kernels, per_device(): pl.pallas_call(functools.partial(kernel, factor), name='mixer_backward',...  161 us

profile of v4, /device:TPU:0, one launch (start us, length us, event | category | flops | bytes accessed | tf_op | source)
XLA Modules:
  0.0 164.0 jit_solution(7828306904117516888)
XLA Ops:
  0.6 160.9 %mixer_backward.1 = (bf16[8,1024,2,128]{3,2,1,0:T(2,128)(2,1)S(1)}, bf16[2,64,768]{2,1,0:T(8,128)(2,1)S(1)}, bf16[2,64,768]{2,1,0:T(8,128)(2,1)S(1)}, bf16[2,48,1024]{2,1,0:T(8,128)(2,1)S(1)}) custom-call(bf16[1024,2,1024]{2,1,0:T(2,128)(2,1)} %x.1, bf16[1024,2,1024]{2,1,0:T(2,128)(2,1)} %g.1, bf16[2,64,768]{2,1,0:T(8,128)(2,1)} %w_gate.1, ...), custom_call_target="tpu_custom_call" | custom-call | tf_op jit(solution)/shard_map/mixer_backward/pallas_call | solution.py:628
  161.5 2.3 %deliver.1 = (bf16[1024,2,1024]{2,1,0:T(2,128)(2,1)}, bf16[2,64,768]{2,1,0:T(8,128)(2,1)}, bf16[2,64,768]{2,1,0:T(8,128)(2,1)}, bf16[2,48,1024]{2,1,0:T(8,128)(2,1)}) custom-call(bf16[8,1024,2,128]{3,2,1,0:T(2,128)(2,1)S(1)} %get-tuple-element.8.blocks, bf16[2,64,768]{2,1,0:T(8,128)(2,1)S(1)} %get-tuple-element.9.gate, ...), custom_call_target="tpu_custom_call" | custom-call | tf_op jit(solution)/shard_map/deliver/pallas_call | solution.py:663

commit v5 on v4

--- a/solution.py
+++ b/solution.py
@@ -131,80 +131,6 @@
     ):
         pl.semaphore_signal(barrier, inc=1, device_id=(me, to), device_id_type=MESH)
     pl.semaphore_signal(barrier, inc=1, device_id=mate, device_id_type=MESH)
-    pl.semaphore_wait(barrier, 12)
-
-    fulls = (full_gate, full_up, full_down)
-    mine = (w_gate, w_up, w_down)
-    relays = (v_gate, v_up, v_down)
-    passing = (u_gate, u_up, u_down)
-    d_c = dp_of(xh, y, 1 - c)
-
-    def gather(token, sends, recvs, shard, to, srcs=None, dsts=None):
-        return [
-            remote(
-                srcs[n] if srcs else fulls[n].at[token, shard],
-                dsts[n] if dsts else fulls[n].at[token, shard],
-                ag_send.at[sends], ag_recv.at[recvs], *to,
-            )
-            for n in range(3)
-        ]
-
-    own = [[ref.at[token] for ref in mine] for token in range(2)]
-    other_core = (me, d_c)
-    first_x = [gather(token, 8 + token, 14 + token, first, mate) for token in range(2)]
-    second_x = (
-        gather(0, 10, 16, second, (inner, d), own[0]),
-        gather(1, 11, 17, second, (inner, d), relays),
-    )
-    second_mate = [gather(token, 12 + token, 18 + token, second, mate) for token in range(2)]
-    relay_x = gather(1, 14, 20, second, mate, own[1], relays)
-
-    def over_y_copies(token, far):
-        shard, at = (first, second)[far], 2 * token + far
-        return [
-            gather(token, at, 3 * at + dy - 1, shard, (me, dp_of(xh, (y + dy) % 4, c))) for dy in (1, 2, 3)
-        ]
-
-    def core_copies(token, far):
-        return gather(token, 2 * token + far, 12 + token, (first, second)[far], other_core)
-
-    def pass_copies(token, far):
-        return [
-            gather(token, 4 + 2 * token + far, 12 + token, dp_of(far, (y + 4 - dy) % 4, c), other_core)
-            for dy in (1, 2, 3)
-        ]
-
-    def start_all(copies):
-        for copy in copies:
-            copy.start()
-
-    def arrived(slot):
-        wait_shards(3, ag_recv.at[slot])
-
-    def spread(token, far):
-        for copies in over_y_copies(token, far):
-            start_all(copies)
-        start_all(core_copies(token, far))
-
-    def pass_on(token, far):
-        for k, onward in enumerate(pass_copies(token, far)):
-            arrived(3 * (2 * token + far) + k)
-            start_all(onward)
-
-    def gathered(token):
-        wait_shards(24, ag_recv.at[12 + token])
-
-    @pl.when(xh == 0)
-    def _():
-        wait_shards(6, wload_sem)
-        start_all(first_x[0])
-        spread(0, 0)
-        start_all(first_x[1])
-
-    @pl.when(xh == 1)
-    def _():
-        start_all(second_x[0])
-        start_all(relay_x)
 
     def incoming(token, which, i):
         return remote(
@@ -231,19 +157,110 @@
 
         lax.fori_loop(0, samples // (ROWS * UNROLL), step, 0)
 
+    @pl.when(xh == 0)
+    def _():
+        shuffle(1, 0)
+
+    pl.semaphore_wait(barrier, 12)
+
+    @pl.when(xh == 0)
+    def _():
+        incoming(0, 0, 1).start()
+
+    fulls = (full_gate, full_up, full_down)
+    mine = (w_gate, w_up, w_down)
+    relays = (v_gate, v_up, v_down)
+    passing = (u_gate, u_up, u_down)
+    d_c = dp_of(xh, y, 1 - c)
+
+    def gather(token, sends, recvs, shard, to, srcs=None, dsts=None):
+        return [
+            remote(
+                srcs[n] if srcs else fulls[n].at[token, shard],
+                dsts[n] if dsts else fulls[n].at[token, shard],
+                ag_send.at[sends], ag_recv.at[recvs], *to,
+            )
+            for n in range(3)
+        ]
+
+    own = [[ref.at[token] for ref in mine] for token in range(2)]
+    other_core = (me, d_c)
+    first_x = [gather(token, 8 + token, 14 + token, first, mate) for token in range(2)]
+    second_x = (
+        gather(0, 10, 16, second, (inner, d), own[0]),
+        gather(1, 11, 17, second, (inner, d), relays),
+    )
+    second_mate = [gather(token, 12 + token, 18 + token, second, mate) for token in range(2)]
+    relay_x = gather(1, 14, 20, second, mate, own[1], relays)
+
+    def over_y_copies(token, far):
+        shard, at = (first, second)[far], 2 * token + far
+        return [
+            gather(token, at, 3 * at + dy - 1, shard, (me, dp_of(xh, (y + dy) % 4, c))) for dy in (1, 2, 3)
+        ]
+
+    def core_copies(token, far):
+        return gather(token, 2 * token + far, 12 + token, (first, second)[far], other_core)
+
+    def pass_copies(token, far):
+        return [
+            gather(token, 4 + 2 * token + far, 12 + token, dp_of(far, (y + 4 - dy) % 4, c), other_core)
+            for dy in (1, 2, 3)
+        ]
+
+    def start_all(copies):
+        for copy in copies:
+            copy.start()
+
+    def arrived(slot):
+        wait_shards(3, ag_recv.at[slot])
+
+    def spread(token, far):
+        for copies in over_y_copies(token, far):
+            start_all(copies)
+        start_all(core_copies(token, far))
+
+    def pass_on(token, far):
+        for k, onward in enumerate(pass_copies(token, far)):
+            arrived(3 * (2 * token + far) + k)
+            start_all(onward)
+
+    def gathered(token):
+        wait_shards(24, ag_recv.at[12 + token])
+
+    @pl.when(xh == 0)
+    def _():
+        wait_shards(6, wload_sem)
+        start_all(first_x[0])
+        spread(0, 0)
+        start_all(first_x[1])
+
+    @pl.when(xh == 1)
+    def _():
+        start_all(second_x[0])
+        start_all(relay_x)
+
     def order(k):
         return jnp.where(k < 2, 1 + 2 * k, jnp.where(k < 5, 2 * k - 2, 2 * k - 5))
 
     def send_in(k, _):
         i = order(k)
-        shuffle(i, 0)
+        ahead = (k == 0) & (xh == 0)
+
+        @pl.when(jnp.logical_not(ahead))
+        def _():
+            shuffle(i, 0)
 
         @pl.when(k > 0)
         def _():
             incoming(0, 1, order(k - 1)).start()
 
         shuffle(i, 1)
-        incoming(0, 0, i).start()
+
+        @pl.when(jnp.logical_not(ahead))
+        def _():
+            incoming(0, 0, i).start()
+
         return 0
 
     lax.fori_loop(0, 5, send_in, 0)
@@ -498,22 +515,22 @@
             wait_shards(24, rs1_send.at[0])
         weight_term(2, token)
         rs1(token, 2).start()
+        backward(token)
+        if token == 1:
+            x_stage(0, 1)
+
+        def send_back(i, _):
+            outgoing(token, i).start()
+            return 0
+
+        lax.fori_loop(1, TOKEN_DEVICES, send_back, 0)
+        own_back(token).start()
+        core_stage(token, 2)
         weight_term(0, token)
         rs1(token, 0).start()
-        core_stage(token, 2)
         weight_term(1, token)
         rs1(token, 1).start()
         core_stage(token, 0)
-        backward(token)
-        if token == 1:
-            x_stage(0, 1)
-
-        def send_back(i, _):
-            outgoing(token, i).start()
-            return 0
-
-        lax.fori_loop(1, TOKEN_DEVICES, send_back, 0)
-        own_back(token).start()
         core_stage(token, 1)
 
     wait_in(0)

time: 164 us -> 162 us (0.988)
  Pallas kernels: 163 us -> 161 us
    pallas_call x1, Pallas kernels: 161 us -> 158 us  [per_device(): pl.pallas_call(functools.partial(kernel, factor), name='mixer_backward',...]
where the time goes in v5:
time: 162 us; the launch traced here: 161 us
  Pallas kernels  161 us (99%)
    pallas_call x1, Pallas kernels, per_device(): pl.pallas_call(functools.partial(kernel, factor), name='mixer_backward',...  158 us

profile of v5, /device:TPU:0, one launch (start us, length us, event | category | flops | bytes accessed | tf_op | source)
XLA Modules:
  0.0 161.5 jit_solution(6340863244354032179)
XLA Ops:
  0.6 158.4 %mixer_backward.1 = (bf16[8,1024,2,128]{3,2,1,0:T(2,128)(2,1)S(1)}, bf16[2,64,768]{2,1,0:T(8,128)(2,1)S(1)}, bf16[2,64,768]{2,1,0:T(8,128)(2,1)S(1)}, bf16[2,48,1024]{2,1,0:T(8,128)(2,1)S(1)}) custom-call(bf16[1024,2,1024]{2,1,0:T(2,128)(2,1)} %x.1, bf16[1024,2,1024]{2,1,0:T(2,128)(2,1)} %g.1, bf16[2,64,768]{2,1,0:T(8,128)(2,1)} %w_gate.1, ...), custom_call_target="tpu_custom_call" | custom-call | tf_op jit(solution)/shard_map/mixer_backward/pallas_call | solution.py:645
  159.1 2.3 %deliver.1 = (bf16[1024,2,1024]{2,1,0:T(2,128)(2,1)}, bf16[2,64,768]{2,1,0:T(8,128)(2,1)}, bf16[2,64,768]{2,1,0:T(8,128)(2,1)}, bf16[2,48,1024]{2,1,0:T(8,128)(2,1)}) custom-call(bf16[8,1024,2,128]{3,2,1,0:T(2,128)(2,1)S(1)} %get-tuple-element.8.blocks, bf16[2,64,768]{2,1,0:T(8,128)(2,1)S(1)} %get-tuple-element.9.gate, ...), custom_call_target="tpu_custom_call" | custom-call | tf_op jit(solution)/shard_map/deliver/pallas_call | solution.py:680

commit v6 on v5

--- a/solution.py
+++ b/solution.py
@@ -430,13 +430,13 @@
 
     def backward(token):
         def step(i, _):
-            r = pl.ds(pl.multiple_of(i * BLOCK, BLOCK), BLOCK)
+            r = pl.ds(pl.multiple_of(i * 2 * BLOCK, 2 * BLOCK), 2 * BLOCK)
             v = (nt(g_gate[r, :], weight(0, token)) + nt(g_up[r, :], weight(1, token))).astype(BF)
             for q in range(TOKEN_DEVICES):
                 stage[token, 0, q, r, :] = v[:, q * LANES : (q + 1) * LANES]
             return 0
 
-        lax.fori_loop(0, samples // BLOCK, step, 0)
+        lax.fori_loop(0, samples // (2 * BLOCK), step, 0)
 
     def core_stage(token, n):
         wait_shards(8, rs1_recv.at[token, n])

time: 162 us -> 162 us (level)
  no operation moved by 1% of the time
where the time goes in v6:
time: 162 us; the launch traced here: 161 us
  Pallas kernels  161 us (99%)
    pallas_call x1, Pallas kernels, per_device(): pl.pallas_call(functools.partial(kernel, factor), name='mixer_backward',...  158 us

profile of v6, /device:TPU:0, one launch (start us, length us, event | category | flops | bytes accessed | tf_op | source)
XLA Modules:
  0.0 161.5 jit_solution(3568336610380653031)
XLA Ops:
  0.6 158.4 %mixer_backward.1 = (bf16[8,1024,2,128]{3,2,1,0:T(2,128)(2,1)S(1)}, bf16[2,64,768]{2,1,0:T(8,128)(2,1)S(1)}, bf16[2,64,768]{2,1,0:T(8,128)(2,1)S(1)}, bf16[2,48,1024]{2,1,0:T(8,128)(2,1)S(1)}) custom-call(bf16[1024,2,1024]{2,1,0:T(2,128)(2,1)} %x.1, bf16[1024,2,1024]{2,1,0:T(2,128)(2,1)} %g.1, bf16[2,64,768]{2,1,0:T(8,128)(2,1)} %w_gate.1, ...), custom_call_target="tpu_custom_call" | custom-call | tf_op jit(solution)/shard_map/mixer_backward/pallas_call | solution.py:645
  159.0 2.3 %deliver.1 = (bf16[1024,2,1024]{2,1,0:T(2,128)(2,1)}, bf16[2,64,768]{2,1,0:T(8,128)(2,1)}, bf16[2,64,768]{2,1,0:T(8,128)(2,1)}, bf16[2,48,1024]{2,1,0:T(8,128)(2,1)}) custom-call(bf16[8,1024,2,128]{3,2,1,0:T(2,128)(2,1)S(1)} %get-tuple-element.8.blocks, bf16[2,64,768]{2,1,0:T(8,128)(2,1)S(1)} %get-tuple-element.9.gate, ...), custom_call_target="tpu_custom_call" | custom-call | tf_op jit(solution)/shard_map/deliver/pallas_call | solution.py:680
